TPU v7x, 128 devices: a whole 4x4x4 slice. The times are simulated.
128 devices in a mesh: col: 64 (over z, y, x_hi, core), seq: 2 (over x_lo).
Axes of the slice: x: 4 (x_hi: 2, x_lo: 2; x = x_hi * 2 + x_lo), y: 4, z: 4, core: 2. Of those that a mesh axis runs over, the one named last changes fastest.
Arguments:
- history_items: int32 [64, 1024], P(None, 'seq'), may hold values from 0 to 65535
- lengths: int32 [64], replicated, may hold values from 64 to 1024, as said below
- item_table: float32 [512, 65536], P('col'), may hold values from -4 to 4
- input_weight: bfloat16 [512, 2048], replicated, may hold values from -0.25 to 0.25
- output_weight: bfloat16 [512, 512], replicated, may hold values from -0.25 to 0.25
- output_cotangent: bfloat16 [64, 1024, 512], P('col', 'seq'), may hold values from -6 to 6
Outputs:
- layer_output: bfloat16 [64, 1024, 512], P('col', 'seq')
- table_gradient: float32 [512, 65536], P('col', 'seq')
Inputs may be any that keep to these rules, and one draw needn't show every extreme that they name: `lengths`: in every draw one history has exactly 1024 items.
All inputs are finite; a program needn't handle non-finite values.
Results may differ from a plain program's by a relative error of at most 0.0077.
Values may be sent and summed in bfloat16 or wider, within the bound.
No kernel may reach another device: no remote copies, remote signals or barrier semaphores. Data moves between devices by JAX's collectives and lax.ppermute only.
A program may use at most 128 MiB of HBM per device.

v0:
```python
import jax
import jax.numpy as jnp
from jax import lax
from jax.sharding import PartitionSpec as P

H = 8
DH = 64
LEN = 1024


norm_epsilon = 1e-05


def joined_along(parts, dim):
    dims = list(parts.shape[1:])
    dims[dim] *= parts.shape[0]
    return jnp.moveaxis(parts, 0, dim).reshape(dims)


def copy_for_each(shard, axis):
    length = lax.axis_size(axis)
    return lax.all_to_all(
        jnp.broadcast_to(shard[None], (length, *shard.shape)), axis, 0, 0, tiled=True
    )


def gathered_copies(shard, axis, dim):
    return joined_along(copy_for_each(shard, axis), dim)


def side_by_side(arrays, axis, dim, along):
    ends, at = ([], 0)
    for a in arrays[:-1]:
        at += a.shape[along]
        ends.append(at)
    both = jnp.concatenate(arrays, axis=along)
    return tuple(jnp.split(gathered_copies(both, axis, dim), ends, axis=along))


def in_blocks(shard, dim, length):
    dims = shard.shape
    parts = shard.reshape(*dims[:dim], length, dims[dim] // length, *dims[dim + 1 :])
    return jnp.moveaxis(parts, dim, 0)


def sum_at_owner(shard, axis, dim):
    parts = in_blocks(shard, dim, lax.axis_size(axis))
    arrived = lax.all_to_all(parts, axis, split_axis=0, concat_axis=0, tiled=True)
    return arrived.sum(axis=0)


def side_by_side_2(arrays, axis, dim, along):
    ends, at = ([], 0)
    for a in arrays[:-1]:
        at += a.shape[along]
        ends.append(at)
    both = jnp.concatenate(arrays, axis=along)
    return tuple(jnp.split(sum_at_owner(both, axis, dim), ends, axis=along))


def layer_norm(inputs):
    average = jnp.mean(inputs, axis=-1, keepdims=True)
    centered = inputs - average
    variance = jnp.mean(centered * centered, axis=-1, keepdims=True)
    return centered * lax.rsqrt(variance + norm_epsilon)


def silu_slope(inputs):
    sigmoid_part = jax.nn.sigmoid(inputs)
    return sigmoid_part * (1.0 + inputs * (1.0 - sigmoid_part))


def per_device(history_items, lengths, item_table, input_weight, output_weight, output_cotangent):
    user_count = history_items.shape[0]
    seq_rows = history_items.shape[1]
    feat_cols = item_table.shape[0]
    hidden = H * DH
    score_scale = DH ** (-0.5)
    length_scale = 1.0 / LEN
    col_index = lax.axis_index("col")
    seq_index = lax.axis_index("seq")
    chosen = jnp.arange(lengths.shape[0], dtype=jnp.int32) == col_index
    length = jnp.sum(jnp.where(chosen, lengths, 0))
    flat_items = history_items.reshape(-1)
    item_major = item_table.T
    looked = (
        jnp.take(item_major, flat_items, axis=0)
        .astype(jnp.bfloat16)
        .reshape(user_count, seq_rows, feat_cols)
    )
    embedded = lax.all_to_all(looked, "col", split_axis=0, concat_axis=2, tiled=True)[0]
    features = embedded.astype(jnp.float32)
    normed = layer_norm(features).astype(jnp.bfloat16)
    preact = jnp.dot(normed, input_weight, preferred_element_type=jnp.float32)
    activated = jax.nn.silu(preact)
    update_part = activated[:, :hidden].astype(jnp.bfloat16)
    value_heads = activated[:, hidden : 2 * hidden].astype(jnp.bfloat16).reshape(seq_rows, H, DH)
    query_heads = (
        activated[:, 2 * hidden : 3 * hidden].astype(jnp.bfloat16).reshape(seq_rows, H, DH)
    )
    key_heads = activated[:, 3 * hidden :].astype(jnp.bfloat16).reshape(seq_rows, H, DH)
    positions = seq_index * seq_rows + jnp.arange(seq_rows, dtype=jnp.int32)
    valid = positions < length
    keys_in, values_in = side_by_side((key_heads, value_heads), "seq", 0, 1)
    remote_pos = jnp.arange(keys_in.shape[0], dtype=jnp.int32)
    allowed = (remote_pos[None, :] <= positions[:, None]) & (remote_pos < length)[None, :]
    scores = (
        jnp.einsum("qhd,khd->hqk", query_heads, keys_in, preferred_element_type=jnp.float32)
        * score_scale
    )
    point_weights = jnp.where(allowed[None], jax.nn.silu(scores) * length_scale, 0.0).astype(
        jnp.bfloat16
    )
    attended = jnp.einsum(
        "hqk,khd->qhd", point_weights, values_in, preferred_element_type=jnp.float32
    ).reshape(seq_rows, hidden)
    normed_att = layer_norm(attended)
    gated = (normed_att * update_part.astype(jnp.float32)).astype(jnp.bfloat16)
    mixed = jnp.dot(gated, output_weight, preferred_element_type=jnp.float32) + features
    layer_output = jnp.where(valid[:, None], mixed, 0.0).astype(jnp.bfloat16)
    grad_row = output_cotangent[0]
    cotangent = jnp.where(valid[:, None], grad_row, jnp.zeros_like(grad_row))
    gated_grad = jnp.dot(cotangent, output_weight.T, preferred_element_type=jnp.float32)
    normed_grad = gated_grad * update_part.astype(jnp.float32)
    update_grad = gated_grad * normed_att
    attended_back = jax.vjp(layer_norm, attended)[1]
    attended_heads = attended_back(normed_grad)[0].astype(jnp.bfloat16).reshape(seq_rows, H, DH)
    keys_in, values_in = side_by_side((key_heads, value_heads), "seq", 0, 1)
    count = keys_in.shape[0]
    remote_pos = jnp.arange(count, dtype=jnp.int32)
    allowed = (remote_pos[None, :] <= positions[:, None]) & (remote_pos < length)[None, :]
    scores = (
        jnp.einsum("qhd,khd->hqk", query_heads, keys_in, preferred_element_type=jnp.float32)
        * score_scale
    )
    point_weights = jnp.where(allowed[None], jax.nn.silu(scores) * length_scale, 0.0).astype(
        jnp.bfloat16
    )
    weight_grad = jnp.einsum(
        "qhd,khd->hqk", attended_heads, values_in, preferred_element_type=jnp.float32
    )
    score_grad = jnp.where(
        allowed[None], weight_grad * silu_slope(scores) * length_scale, 0.0
    ).astype(jnp.bfloat16)
    query_grad = jnp.einsum("hqk,khd->qhd", score_grad, keys_in, preferred_element_type=jnp.float32)
    key_part = jnp.einsum(
        "hqk,qhd->khd", score_grad, query_heads, preferred_element_type=jnp.float32
    )
    value_part = jnp.einsum(
        "hqk,qhd->khd", point_weights, attended_heads, preferred_element_type=jnp.float32
    )
    key_whole = key_part
    value_whole = value_part
    query_grad, key_whole, value_whole = (query_grad, key_whole, value_whole)
    key_grad, value_grad = side_by_side_2((key_whole, value_whole), "seq", 0, 1)
    query_grad = query_grad * score_scale
    key_grad = key_grad * score_scale
    activation_grad = jnp.concatenate(
        [
            update_grad,
            value_grad.reshape(seq_rows, hidden),
            query_grad.reshape(seq_rows, hidden),
            key_grad.reshape(seq_rows, hidden),
        ],
        axis=-1,
    )
    preact_grad = (activation_grad * silu_slope(preact)).astype(jnp.bfloat16)
    entry_grad = jnp.dot(preact_grad, input_weight.T, preferred_element_type=jnp.float32)
    features_back = jax.vjp(layer_norm, features)[1]
    input_grad = cotangent.astype(jnp.float32) + features_back(entry_grad)[0]
    back_rows = lax.all_to_all(
        input_grad[None], "col", split_axis=2, concat_axis=0, tiled=True
    ).reshape(-1, feat_cols)
    dense_grad = (
        jnp.zeros((item_table.shape[1], feat_cols), jnp.float32).at[flat_items].add(back_rows)
    )
    table_gradient = sum_at_owner(dense_grad.T, "seq", 1)
    return (layer_output[None], table_gradient)


def solution(mesh):
    in_specs = (P(None, "seq"), P(), P("col", None), P(), P(), P("col", "seq", None))
    out_specs = (P("col", "seq", None), P("col", "seq"))
    return jax.shard_map(
        per_device, mesh=mesh, in_specs=in_specs, out_specs=out_specs, check_vma=False
    )
```

profile of v0, /device:TPU:1, one launch (start us, length us, event | category | flops | bytes accessed | tf_op | source)
XLA Modules:
  0.0 607.7 jit_solution(5730726453310579316)
XLA Ops:
  0.6 1.1 compare_and_fusion
  1.7 1.0 copy.86
  3.6 12.0 %copy.57 = bf16[8,65536]{0,1:T(8,128)(2,1)} copy(f32[8,65536]{1,0:T(8,128)} %param.8) | data formatting | bytes 3145728 | tf_op args[2]
  15.6 117.3 %gather_fusion = bf16[32768,8]{1,0:T(8,128)(2,1)} fusion(bf16[65536,8]{1,0:T(8,128)(2,1)} %bitcast.81, s32[32768]{0:T(1024)S(1)} %broadcast_clamp_fusion), kind=kCustom, calls=%fused_computation | custom fusion | bytes 1179648 | tf_op jit(solution)/shard_map/jit(_take)/gather | solution.py:87
  132.8 5.9 copy.58
  139.0 26.5 %all_to_all.40 = bf16[64,512,8]{1,2,0:T(8,128)(2,1)S(1)} all-to-all(bf16[64,512,8]{1,2,0:T(8,128)(2,1)S(1)} %select_convert_fusion.2), channel_id=1, replica_groups=mesh['col'=64,'seq'=2] {'col'}, dimensions={0} | all-to-all | bytes 1048576 | tf_op jit(solution)/shard_map/all_to_all | solution.py:91
  165.8 1.1 convert_bitcast_fusion
  166.9 1.6 copy.59
  168.5 3.6 multiply_convert_fusion
  172.1 1.3 copy-done.5
  174.4 2.1 copy.61
  177.4 1.3 pad_maximum_fusion.1
  178.7 1.6 broadcast_in_dim.110
  180.3 5.3 all-to-all-start.1
  187.6 1.2 fusion.3
  189.1 21.1 %all-to-all-done.1 = bf16[2,512,16,64]{1,3,2,0:T(8,128)(2,1)} async-done(((bf16[2,512,16,64]{1,3,2,0:T(8,128)(2,1)}), bf16[2,512,16,64]{1,3,2,0:T(8,128)(2,1)}, u32[]{:S(2)}, u32[]{:S(2)}) %all-to-all-start.1) | async-done | bytes 2097184 | tf_op jit(solution)/shard_map/all_to_all | solution.py:22
  210.2 1.8 copy.85
  212.1 9.6 %select_convert_fusion.1 = (bf16[8,512,1024]{2,1,0:T(8,128)(2,1)S(1)}, f32[8,512,1024]{2,1,0:T(8,128)}) fusion(pred[512,1024]{1,0:T(8,128)(4,1)S(1)} %copy-done.13, bf16[512,8,64]{0,2,1:T(8,128)(2,1)S(1)} %bitcast.91, bf16[1024,16,64]{0,2,1:T(8,128)(2,1)S(1)} %bitcast.95), kind=kOutput, calls=%fused_computation.5 | convolution fusion | flops 570425344 | bytes 27262976 | tf_op jit(solution)/shard_map/qhd,khd->hqk/dot_general | solution.py:108
  221.7 2.7 fusion.36
  225.9 1.6 copy.64
  227.4 2.0 multiply_reduce_fusion.1
  229.5 2.5 fusion.33
  232.9 2.0 copy.68
  235.0 5.3 convolution_bitcast_fusion
  240.3 11.6 %select_convert_fusion = bf16[8,512,1024]{2,1,0:T(8,128)(2,1)S(1)} fusion(f32[8,512,1024]{2,1,0:T(8,128)} %get-tuple-element.19, bf16[512,8,64]{0,2,1:T(8,128)(2,1)S(1)} %bitcast.94, pred[512,1024]{1,0:T(8,128)(4,1)S(1)} %copy-done.14, bf16[1024,16,64]{0,2,1:T(8,128)(2,1)S(1)} %bitcast.98), kind=kOutput, calls=%fused_computation.2 | convolution fusion | flops 587202560 | bytes 27262976 | tf_op jit(solution)/shard_map/qhd,khd->hqk/dot_general | solution.py:139
  251.9 1.6 convolution_bitcast_fusion.1
  253.5 1.6 copy-done.2
  255.4 2.4 copy.88
  257.9 5.7 all-to-all-start.2
  263.5 7.4 %convolution_multiply_fusion = f32[8,64,512]{2,1,0:T(8,128)} fusion(bf16[1024,16,64]{0,2,1:T(8,128)(2,1)} %bitcast.97, bf16[8,512,1024]{2,1,0:T(8,128)(2,1)} %copy-done.2), kind=kOutput, calls=%fused_computation.25 | convolution fusion | flops 537133056 | bytes 11534336 | tf_op jit(solution)/shard_map/hqk,khd->qhd/dot_general | solution.py:145
  270.9 2.6 copy.71
  273.5 36.2 %all-to-all-done.2 = f32[2,512,16,64]{1,3,2,0:T(8,128)} async-done(((f32[2,512,16,64]{1,3,2,0:T(8,128)}), f32[2,512,16,64]{1,3,2,0:T(8,128)}, u32[]{:S(2)}, u32[]{:S(2)}) %all-to-all-start.2) | async-done | bytes 4194336 | tf_op jit(solution)/shard_map/all_to_all | solution.py:48
  309.7 4.2 reduce_sum.107
  313.9 3.1 fusion.34
  317.0 2.5 copy.70
  319.6 2.6 copy.72
  322.1 5.8 multiply_reduce_fusion
  328.4 1.2 add_bitcast_fusion
  329.6 3.6 copy.75
  333.2 26.4 %all_to_all.41 = f32[1,512,512]{1,0,2:T(1,128)S(1)} all-to-all(f32[1,512,512]{1,0,2:T(1,128)} %copy.75), channel_id=1, replica_groups=mesh['col'=64,'seq'=2] {'col'}, dimensions={2} | all-to-all | bytes 2097152 | tf_op jit(solution)/shard_map/all_to_all | solution.py:171
  359.7 1.1 copy.82
  360.8 9.1 %copy.76 = f32[32768,8]{1,0:T(8,128)} copy(f32[32768,8]{0,1:T(8,128)} %bitcast.87) | data formatting | bytes 2097152 | tf_op jit(solution)/shard_map/reshape | solution.py:173
  369.8 187.3 %scatter_custom_fusion = f32[65536,8]{1,0:T(8,128)} fusion(s32[32768]{0:T(1024)} %bitcast.104, f32[32768,8]{1,0:T(8,128)} %copy.76, f32[]{:T(128)} %constant.53.clone.1), kind=kCustom, calls=%fused_computation.3 | custom fusion | flops 262144 | bytes 2097664 | tf_op jit(solution)/shard_map/scatter-add | solution.py:175
  557.2 18.2 %copy.77 = f32[8,2,32768]{2,0,1:T(8,128)} copy(f32[8,2,32768]{0,2,1:T(8,128)} %bitcast.82) | data formatting | bytes 4194304 | tf_op jit(solution)/shard_map/reshape | solution.py:42
  575.4 4.8 all-to-all-start.4
  580.2 2.8 fusion.8
  583.0 21.6 %all-to-all-done.4 = f32[2,8,32768]{2,1,0:T(8,128)} async-done(((f32[2,8,32768]{2,1,0:T(8,128)}), f32[2,8,32768]{2,1,0:T(8,128)}, u32[]{:S(2)}, u32[]{:S(2)}) %all-to-all-start.4) | async-done | bytes 2097184 | tf_op jit(solution)/shard_map/all_to_all | solution.py:48
  604.6 2.8 reduce_sum.113
  (55 shorter events, 8.6 us)
Async XLA Ops:
  0.6 167.8 %copy-start = (bf16[512,2048]{1,0:T(8,128)(2,1)S(1)}, bf16[512,2048]{1,0:T(8,128)(2,1)}, u32[]{:S(2)}) copy-start(bf16[512,2048]{1,0:T(8,128)(2,1)} %param.9) | copy-start | bytes 6291460
  2.9 0.6 copy-start.15
  168.5 3.6 copy-start.3
  172.1 1.3 copy-start.5
  178.7 6.9 %copy-start.16 = (s32[64]{0:T(128)S(1)}, s32[64]{0:T(128)}, u32[]{:S(2)}) copy-start(s32[64]{0:T(128)} %param.7) | copy-start | bytes 772
  180.3 29.9 %all-to-all-start.1 = ((bf16[2,512,16,64]{1,3,2,0:T(8,128)(2,1)}), bf16[2,512,16,64]{1,3,2,0:T(8,128)(2,1)}, u32[]{:S(2)}, u32[]{:S(2)}) async-start(bf16[2,512,16,64]{1,3,2,0:T(8,128)(2,1)} %broadcast_in_dim.110), calls=%async_computation.1 | async-start | bytes 4194304 | tf_op jit(solution)/shard_map/all_to_all | solution.py:22
  189.1 32.6 %copy-start.7 = (bf16[512,512]{0,1:T(8,128)(2,1)}, bf16[512,512]{0,1:T(8,128)(2,1)S(1)}, u32[]{:S(2)}) copy-start(bf16[512,512]{0,1:T(8,128)(2,1)S(1)} %copy.63) | copy-start | bytes 1572868
  189.1 23.0 %copy-start.13 = (pred[512,1024]{1,0:T(8,128)(4,1)S(1)}, pred[512,1024]{1,0:T(8,128)(4,1)}, u32[]{:S(2)}) copy-start(pred[512,1024]{1,0:T(8,128)(4,1)} %fusion.3) | copy-start | bytes 1572868
  212.0 9.6 %copy-start.11 = (bf16[2,16,8,8,512]{4,3,0,2,1:T(8,128)(2,1)}, bf16[2,16,8,8,512]{4,3,0,2,1:T(8,128)(2,1)S(1)}, u32[]{:S(2)}) copy-start(bf16[2,16,8,8,512]{4,3,0,2,1:T(8,128)(2,1)S(1)} %copy.85) | copy-start | bytes 6291460
  221.7 3.2 copy-start.1
  224.9 1.0 copy-start.6
  235.0 5.3 copy-start.9
  235.0 5.3 copy-start.12
  235.0 5.3 copy-start.14
  240.3 11.6 %copy-start.8 = (bf16[512,512]{0,1:T(8,128)(2,1)S(1)}, bf16[512,512]{0,1:T(8,128)(2,1)}, u32[]{:S(2)}) copy-start(bf16[512,512]{0,1:T(8,128)(2,1)} %copy-done.7) | copy-start | bytes 1572868
  251.9 3.2 copy-start.2
  257.9 51.8 %all-to-all-start.2 = ((f32[2,512,16,64]{1,3,2,0:T(8,128)}), f32[2,512,16,64]{1,3,2,0:T(8,128)}, u32[]{:S(2)}, u32[]{:S(2)}) async-start(f32[2,512,16,64]{1,3,2,0:T(8,128)} %bitcast.84), calls=%async_computation.2 | async-start | bytes 8388608 | tf_op jit(solution)/shard_map/all_to_all | solution.py:48
  322.1 5.9 copy-start.4
  322.1 6.3 %copy-start.10 = (bf16[1,512,512]{2,1,0:T(8,128)(2,1)S(1)}, bf16[1,512,512]{2,1,0:T(8,128)(2,1)}, u32[]{:S(2)}) copy-start(bf16[1,512,512]{2,1,0:T(8,128)(2,1)} %param.11) | copy-start | bytes 1572868
  575.4 29.3 %all-to-all-start.4 = ((f32[2,8,32768]{2,1,0:T(8,128)}), f32[2,8,32768]{2,1,0:T(8,128)}, u32[]{:S(2)}, u32[]{:S(2)}) async-start(f32[2,8,32768]{2,1,0:T(8,128)} %bitcast.86), calls=%async_computation.4 | async-start | bytes 4194304 | tf_op jit(solution)/shard_map/all_to_all | solution.py:48
where the time goes:
time: 615 us; the launch traced here: 608 us
  other arithmetic  210 us (34%)
  local copies, waits for them, and re-layouts  196 us (32%)
  waiting for transfers between devices  78.9 us (13%)
  blocking collectives  53 us (9%)
  matrix products  52.4 us (9%)
  starting transfers between devices  15.8 us (3%)
    scatter-add x1, other arithmetic, per_device(): jnp.zeros((item_table.shape[1], feat_cols), jnp.float32).at[flat_items]  187 us
    gather x2, local copies, waits for them, and re-layouts, per_device(): jnp.take(item_major, flat_items, axis=0).astype(jnp.bfloat16)  123 us
    all_to_all x2, waiting for transfers between devices, sum_at_owner(): lax.all_to_all(parts, axis, split_axis=0, concat_axis=0, tiled=True)  57.8 us
    all_to_all x1, blocking collectives, per_device(): lax.all_to_all(looked, 'col', split_axis=0, concat_axis=2, tiled=True)[0]  26.5 us
    all_to_all x1, blocking collectives, per_device(): lax.all_to_all(input_grad[None], 'col', split_axis=2, concat_axis=0, tile...  26.4 us
    all_to_all x1, waiting for transfers between devices, copy_for_each(): lax.all_to_all(jnp.broadcast_to(shard[None], (length, *shard.shape)), axi...  21.1 us
    reshape x2, local copies, waits for them, and re-layouts, in_blocks(): shard.reshape(*dims[:dim], length, dims[dim] // length, *dims[dim + 1:])  20.6 us
    unnamed x37, local copies, waits for them, and re-layouts  19 us
  transfers between devices with their start and end apart: 3, of which 3 were waited for; matrix products, arithmetic and copies ran while one was open for 3% of the time, Pallas kernels for 0%

commit v1 on v0

v1 whole, which is shorter than its diff:
```python
import jax
import jax.numpy as jnp
from jax import lax
from jax.experimental import pallas as pl
from jax.experimental.pallas import tpu as pltpu
from jax.sharding import PartitionSpec as P

H = 8
DH = 64
LEN = 1024
D = 512
HID = H * DH
USERS = 64
FEAT = 8
HALF = 512
BLK = 128
NBLK = HALF // BLK
ROWS = 65536
PAIRS = H // 2
norm_epsilon = 1e-05
bf16 = jnp.bfloat16
f32 = jnp.float32

G_LO = 32
G_HI = ROWS // G_LO
G_STEP = 8
S_ROWS = ROWS // 2
S_LO = 32
S_HI = S_ROWS // S_LO
S_STEP = 16


def block_list(meta_ref, list_ref):
    seq = meta_ref[0]

    def step(u, count):
        parity = (seq + u) & 1
        blocks = (meta_ref[2 + u] + (BLK - 1)) // BLK
        for i in range(NBLK):
            list_ref[count + i] = u * NBLK + i
        return count + (blocks + 1 - parity) // 2

    return lax.fori_loop(0, USERS, step, 0)


def item_row(items_ref, seq, block):
    u = block // NBLK
    i = block % NBLK
    parity = (seq + u) & 1
    half = i // 2
    row = half * (USERS * NBLK) + u * NBLK + 2 * (i % 2) + parity
    return items_ref[pl.ds(row, 1), :]


def stage_items(seq, own_ref, other_ref, items_ref):
    n = USERS * NBLK
    items_ref[pl.ds(pl.multiple_of(seq * n, n), n), :] = own_ref[...]
    items_ref[pl.ds(pl.multiple_of((1 - seq) * n, n), n), :] = other_ref[...]


def onehot(index, rows):
    n = index.shape[1]
    iota = lax.broadcasted_iota(jnp.int16, (rows, n), 0)
    wide = jnp.broadcast_to(index.astype(jnp.int16), (rows, n))
    return jnp.where(iota == wide, jnp.ones((), bf16), jnp.zeros((), bf16))


def gather_kernel(meta_ref, own_ref, other_ref, table_ref, out_ref, t_ref, items_ref, list_ref):
    seq = meta_ref[0]
    stage_items(seq, own_ref, other_ref, items_ref)
    for lo in range(G_LO):
        t_ref[lo * FEAT : (lo + 1) * FEAT, :] = table_ref[:, lo * G_HI : (lo + 1) * G_HI].astype(bf16)
    out_ref[...] = jnp.zeros_like(out_ref)
    count = block_list(meta_ref, list_ref)

    def step(g, carry):
        ids = []
        for j in range(G_STEP):
            b = jnp.minimum(g * G_STEP + j, count - 1)
            ids.append(list_ref[jnp.maximum(b, 0)])
        index = jnp.concatenate([item_row(items_ref, seq, b) for b in ids], axis=1)
        lo = lax.shift_right_logical(index, 11)
        hi = index & (G_HI - 1)
        acc = jnp.dot(t_ref[...], onehot(hi, G_HI), preferred_element_type=f32)
        n = G_STEP * BLK
        acc = acc.reshape(G_LO, FEAT, n)
        mask = lax.broadcasted_iota(jnp.int32, (G_LO, FEAT, n), 0) == lo.reshape(1, 1, n)
        picked = jnp.sum(jnp.where(mask, acc, 0.0), axis=0).astype(bf16)
        for j in range(G_STEP):
            u = ids[j] // NBLK
            col = pl.multiple_of((ids[j] % NBLK) * BLK, BLK)
            part = picked[:, j * BLK : (j + 1) * BLK]
            out_ref[u, 0, :, pl.ds(col, BLK)] = part
            out_ref[u, 1, :, pl.ds(col, BLK)] = part
        return carry

    lax.fori_loop(0, (count + G_STEP - 1) // G_STEP, step, 0)


def scatter_kernel(meta_ref, half_ref, own_ref, other_ref, grad_ref, out_ref, items_ref, acc_ref, list_ref):
    seq = meta_ref[0]
    base = half_ref[0] * S_ROWS
    stage_items(seq, own_ref, other_ref, items_ref)
    acc_ref[...] = jnp.zeros_like(acc_ref)
    count = block_list(meta_ref, list_ref)

    def step(g, carry):
        rows, grads = [], []
        for j in range(S_STEP):
            at = g * S_STEP + j
            b = list_ref[jnp.maximum(jnp.minimum(at, count - 1), 0)]
            row = item_row(items_ref, seq, b) - base
            rows.append(jnp.where(at < count, row, -1))
            u = b // NBLK
            col = pl.multiple_of((b % NBLK) * BLK, BLK)
            grads.append(
                grad_ref[u, 0, :, pl.ds(col, BLK)].astype(f32)
                + grad_ref[u, 1, :, pl.ds(col, BLK)].astype(f32)
            )
        index = jnp.concatenate(rows, axis=1)
        grad = jnp.concatenate(grads, axis=1)
        n = S_STEP * BLK
        lo = lax.shift_right_arithmetic(index, 10)
        hi = index & (S_HI - 1)
        mask = lax.broadcasted_iota(jnp.int32, (S_LO, FEAT, n), 0) == lo.reshape(1, 1, n)
        spread = jnp.where(mask, jnp.broadcast_to(grad[None], (S_LO, FEAT, n)), 0.0)
        spread = spread.reshape(S_LO * FEAT, n).astype(bf16)
        acc_ref[...] += lax.dot_general(
            spread, onehot(hi, S_HI), (((1,), (1,)), ((), ())), preferred_element_type=f32
        )
        return carry

    lax.fori_loop(0, (count + S_STEP - 1) // S_STEP, step, 0)
    for lo in range(S_LO):
        out_ref[:, lo * S_HI : (lo + 1) * S_HI] = acc_ref[lo * FEAT : (lo + 1) * FEAT, :].astype(
            out_ref.dtype
        )


def dot_nt(a, b):
    return lax.dot_general(a, b, (((1,), (1,)), ((), ())), preferred_element_type=f32)


def dot_tn(a, b):
    return lax.dot_general(a, b, (((0,), (0,)), ((), ())), preferred_element_type=f32)


def dot_nn(a, b):
    return jnp.dot(a, b, preferred_element_type=f32)


def norm(z):
    m = jnp.mean(z, axis=-1, keepdims=True)
    c = z - m
    w = jnp.mean(c * c, axis=-1, keepdims=True)
    r = lax.rsqrt(w + norm_epsilon)
    return c * r, r


def norm_back(y, r, dy):
    a = jnp.mean(dy, axis=-1, keepdims=True)
    b = jnp.mean(dy * y, axis=-1, keepdims=True)
    return r * (dy - a - y * b)


def sigmoid(x):
    return 0.5 * jnp.tanh(0.5 * x) + 0.5


def layer_kernel(
    meta_ref, e_ref, w_ref, wo_ref, cot_ref, out_ref, g_ref,
    x_ref, y_ref, r_ref, yl_ref, rl_ref, slope_ref, slopel_ref, u_ref, q_ref, k_ref, v_ref,
    p_ref, d_ref, pl_ref, dl_ref, att_ref, do_ref, pg_ref, pgl_ref,
):
    seq = meta_ref[0]
    col = meta_ref[1]
    length = meta_ref[2 + col]
    base = seq * HALF
    upper = seq == 1
    active = length > base
    lanes = lax.broadcasted_iota(jnp.int32, (1, 2 * DH), 1)
    head_mask = [(lanes < DH).astype(f32).astype(bf16), (lanes >= DH).astype(f32).astype(bf16)]

    def place(half, b):
        i = 2 * half + b // 2
        return (b + col) & 1, pl.multiple_of(i * BLK, BLK)

    def features(half):
        parts = []
        for b in range(NBLK):
            src, at = place(half, b)
            part = e_ref[:, src, :, pl.ds(at, BLK)].astype(f32).reshape(D, BLK)
            parts.append(part.T)
        return jnp.concatenate(parts, axis=0)

    def put_grad(half, grad):
        flat = grad.T.reshape(D // FEAT, FEAT, HALF).astype(bf16)
        for b in range(NBLK):
            dst, at = place(half, b)
            g_ref[:, dst, :, pl.ds(at, BLK)] = flat[:, :, b * BLK : (b + 1) * BLK]

    def activate(pre):
        s = sigmoid(pre)
        act = pre * s
        return act, s + act * (1.0 - s)

    g_ref[...] = jnp.zeros_like(g_ref)

    @pl.when(jnp.logical_not(active))
    def _():
        out_ref[...] = jnp.zeros_like(out_ref)

    @pl.when(active)
    def _():
        x = features(seq)
        x_ref[...] = x
        y, r = norm(x)
        y_ref[...] = y
        r_ref[...] = r
        yb = y.astype(bf16)
        for blk in range(4):
            act, slope = activate(dot_nn(yb, w_ref[:, blk * HID : (blk + 1) * HID]))
            slope_ref[:, blk * HID : (blk + 1) * HID] = slope
            if blk == 2:
                act = act.astype(bf16).astype(f32) * (DH**-0.5)
            act = act.astype(bf16)
            if blk == 0:
                u_ref[...] = act
            else:
                for hp in range(PAIRS):
                    part = act[:, hp * 2 * DH : (hp + 1) * 2 * DH]
                    if blk == 1:
                        v_ref[1, hp] = part
                    elif blk == 2:
                        q_ref[hp] = part
                    else:
                        k_ref[1, hp] = part

        @pl.when(upper)
        def _():
            y, r = norm(features(0))
            yl_ref[...] = y
            rl_ref[...] = r
            yb = y.astype(bf16)
            for n, blk in enumerate((1, 3)):
                act, slope = activate(dot_nn(yb, w_ref[:, blk * HID : (blk + 1) * HID]))
                slopel_ref[:, n * HID : (n + 1) * HID] = slope
                act = act.astype(bf16)
                for hp in range(PAIRS):
                    part = act[:, hp * 2 * DH : (hp + 1) * 2 * DH]
                    if n == 0:
                        v_ref[0, hp] = part
                    else:
                        k_ref[0, hp] = part

        def weights(scores, limit):
            s = sigmoid(scores)
            act = scores * s
            slope = s + act * (1.0 - s)
            if limit is not None:
                ok = lax.broadcasted_iota(jnp.int32, scores.shape, 1) <= limit
                act = jnp.where(ok, act, 0.0)
                slope = jnp.where(ok, slope, 0.0)
            return (act * (1.0 / LEN)).astype(bf16), slope * (1.0 / LEN)

        QB = HALF // 2
        row = lax.broadcasted_iota(jnp.int32, (QB, 1), 0)

        @pl.loop(0, PAIRS)
        def _(hp):
            q, k, v = q_ref[hp], k_ref[1, hp], v_ref[1, hp]
            att = [None, None]
            for h in range(2):
                vm = v * head_mask[h]
                for qi in range(2):
                    qb = q[qi * QB : (qi + 1) * QB] * head_mask[h]
                    for ki in range(qi + 1):
                        scores = dot_nt(qb, k[ki * QB : (ki + 1) * QB])
                        limit = None
                        if ki == qi:
                            limit = jnp.minimum(row, length - 1 - base - ki * QB)
                        p, d = weights(scores, limit)
                        at = 2 * qi + ki
                        p_ref[2 * hp + h, at] = p
                        d_ref[2 * hp + h, at] = d
                        add = dot_nn(p, vm[ki * QB : (ki + 1) * QB])
                        att[qi] = add if att[qi] is None else att[qi] + add
            att_ref[hp] = jnp.concatenate(att, axis=0)

            @pl.when(upper)
            def _():
                kl, vl = k_ref[0, hp], v_ref[0, hp]
                for h in range(2):
                    scores = dot_nt(q * head_mask[h], kl)
                    p, d = weights(scores, None)
                    pl_ref[2 * hp + h] = p
                    dl_ref[2 * hp + h] = d
                    att_ref[hp] += dot_nn(p, vl * head_mask[h])

        att = jnp.concatenate([att_ref[hp] for hp in range(PAIRS)], axis=1)
        na, ra = norm(att)
        u = u_ref[...].astype(f32)
        valid = (base + lax.broadcasted_iota(jnp.int32, (HALF, 1), 0)) < length
        mixed = dot_nn((na * u).astype(bf16), wo_ref[...]) + x_ref[...]
        out_ref[...] = jnp.where(valid, mixed, 0.0).astype(bf16)
        cot = jnp.where(valid, cot_ref[...].astype(f32), 0.0)
        gg = dot_nt(cot.astype(bf16), wo_ref[...])
        pg_ref[:, :HID] = (gg * na * slope_ref[:, :HID]).astype(bf16)
        da = norm_back(na, ra, gg * u).astype(bf16)
        for hp in range(PAIRS):
            do_ref[hp] = da[:, hp * 2 * DH : (hp + 1) * 2 * DH]

        @pl.loop(0, PAIRS)
        def _(hp):
            q, k, v, do = q_ref[hp], k_ref[1, hp], v_ref[1, hp], do_ref[hp]
            dq = [None, None]
            dk = [None, None]
            dv = [None, None]

            def plus(a, b):
                return b if a is None else a + b

            for h in range(2):
                km = k * head_mask[h]
                qm = q * head_mask[h]
                dm = do * head_mask[h]
                for qi in range(2):
                    qs = slice(qi * QB, (qi + 1) * QB)
                    for ki in range(qi + 1):
                        ks = slice(ki * QB, (ki + 1) * QB)
                        at = 2 * qi + ki
                        ds = (dot_nt(dm[qs], v[ks]) * d_ref[2 * hp + h, at]).astype(bf16)
                        dq[qi] = plus(dq[qi], dot_nn(ds, km[ks]))
                        dk[ki] = plus(dk[ki], dot_tn(ds, qm[qs]))
                        dv[ki] = plus(dv[ki], dot_tn(p_ref[2 * hp + h, at], dm[qs]))
            at = pl.multiple_of(hp * 2 * DH, 2 * DH)
            vs = pl.ds(HID + at, 2 * DH)
            qs_ = pl.ds(2 * HID + at, 2 * DH)
            ks_ = pl.ds(3 * HID + at, 2 * DH)
            pg_ref[:, vs] = (jnp.concatenate(dv, axis=0) * slope_ref[:, vs]).astype(bf16)
            pg_ref[:, ks_] = (jnp.concatenate(dk, axis=0) * slope_ref[:, ks_]).astype(bf16)
            att_ref[hp] = jnp.concatenate(dq, axis=0)

            @pl.when(upper)
            def _():
                kl, vl = k_ref[0, hp], v_ref[0, hp]
                dkl, dvl = None, None
                for h in range(2):
                    dm = do * head_mask[h]
                    ds = (dot_nt(dm, vl) * dl_ref[2 * hp + h]).astype(bf16)
                    att_ref[hp] += dot_nn(ds, kl * head_mask[h])
                    dkl = plus(dkl, dot_tn(ds, q * head_mask[h]))
                    dvl = plus(dvl, dot_tn(pl_ref[2 * hp + h], dm))
                vl_ = pl.ds(at, 2 * DH)
                kl_ = pl.ds(HID + at, 2 * DH)
                pgl_ref[:, vl_] = (dvl * slopel_ref[:, vl_]).astype(bf16)
                pgl_ref[:, kl_] = (dkl * slopel_ref[:, kl_]).astype(bf16)

            pg_ref[:, qs_] = (att_ref[hp] * (DH**-0.5) * slope_ref[:, qs_]).astype(bf16)

        eg = dot_nt(pg_ref[...], w_ref[...])
        cot = jnp.where(valid, cot_ref[...].astype(f32), 0.0)
        put_grad(seq, cot + norm_back(y_ref[...], r_ref[...], eg))

        @pl.when(upper)
        def _():
            eg = dot_nt(pgl_ref[:, :HID], w_ref[:, HID : 2 * HID])
            eg = eg + dot_nt(pgl_ref[:, HID:], w_ref[:, 3 * HID :])
            put_grad(0, norm_back(yl_ref[...], rl_ref[...], eg))


def vmem():
    return pl.BlockSpec(memory_space=pltpu.VMEM)


def smem():
    return pl.BlockSpec(memory_space=pltpu.SMEM)


def params():
    return pltpu.CompilerParams(vmem_limit_bytes=60 * 1024 * 1024)


def gather(meta, own, other, table):
    return pl.pallas_call(
        gather_kernel,
        in_specs=[smem(), vmem(), vmem(), vmem()],
        out_specs=vmem(),
        out_shape=jax.ShapeDtypeStruct((USERS, 2, FEAT, HALF), bf16),
        scratch_shapes=[
            pltpu.VMEM((G_LO * FEAT, G_HI), bf16),
            pltpu.VMEM((2 * USERS * NBLK, BLK), jnp.int32),
            pltpu.SMEM((USERS * NBLK + NBLK,), jnp.int32),
        ],
        compiler_params=params(),
        name="gather",
    )(meta, own, other, table)


def scatter(meta, half, own, other, grad, dtype):
    return pl.pallas_call(
        scatter_kernel,
        in_specs=[smem(), smem(), vmem(), vmem(), vmem()],
        out_specs=vmem(),
        out_shape=jax.ShapeDtypeStruct((FEAT, S_ROWS), dtype),
        scratch_shapes=[
            pltpu.VMEM((2 * USERS * NBLK, BLK), jnp.int32),
            pltpu.VMEM((S_LO * FEAT, S_HI), f32),
            pltpu.SMEM((USERS * NBLK + NBLK,), jnp.int32),
        ],
        compiler_params=params(),
        name="scatter",
    )(meta, half, own, other, grad)


def layer(meta, e, w, wo, cot):
    return pl.pallas_call(
        layer_kernel,
        in_specs=[smem(), vmem(), vmem(), vmem(), vmem()],
        out_specs=(vmem(), vmem()),
        out_shape=(
            jax.ShapeDtypeStruct((HALF, D), bf16),
            jax.ShapeDtypeStruct((USERS, 2, FEAT, HALF), bf16),
        ),
        scratch_shapes=[
            pltpu.VMEM((HALF, D), f32),
            pltpu.VMEM((HALF, D), f32),
            pltpu.VMEM((HALF, 1), f32),
            pltpu.VMEM((HALF, D), f32),
            pltpu.VMEM((HALF, 1), f32),
            pltpu.VMEM((HALF, 4 * HID), f32),
            pltpu.VMEM((HALF, 2 * HID), f32),
            pltpu.VMEM((HALF, HID), bf16),
            pltpu.VMEM((PAIRS, HALF, 2 * DH), bf16),
            pltpu.VMEM((2, PAIRS, HALF, 2 * DH), bf16),
            pltpu.VMEM((2, PAIRS, HALF, 2 * DH), bf16),
            pltpu.VMEM((H, 4, HALF // 2, HALF // 2), bf16),
            pltpu.VMEM((H, 4, HALF // 2, HALF // 2), f32),
            pltpu.VMEM((H, HALF, HALF), bf16),
            pltpu.VMEM((H, HALF, HALF), f32),
            pltpu.VMEM((PAIRS, HALF, 2 * DH), f32),
            pltpu.VMEM((PAIRS, HALF, 2 * DH), bf16),
            pltpu.VMEM((HALF, 4 * HID), bf16),
            pltpu.VMEM((HALF, 2 * HID), bf16),
        ],
        compiler_params=params(),
        name="layer",
    )(meta, e, w, wo, cot)


def per_device(history_items, lengths, item_table, input_weight, output_weight, output_cotangent):
    col = lax.axis_index("col").astype(jnp.int32)
    seq = lax.axis_index("seq").astype(jnp.int32)
    meta = jnp.concatenate([jnp.stack([seq, col]), lengths])
    own = history_items.reshape(USERS * NBLK, BLK)
    other = lax.ppermute(own, "seq", [(0, 1), (1, 0)])
    looked = gather(meta, own, other, item_table)
    both = ("col", "seq")
    flat = looked.reshape(2 * USERS, FEAT, HALF)
    arrived = lax.all_to_all(flat, both, split_axis=0, concat_axis=0, tiled=True)
    arrived = arrived.reshape(USERS, 2, FEAT, HALF)
    out, grad = layer(meta, arrived, input_weight, output_weight, output_cotangent[0])
    grad = grad.reshape(2 * USERS, FEAT, HALF)
    back = lax.all_to_all(grad, both, split_axis=0, concat_axis=0, tiled=True)
    back = back.reshape(USERS, 2, FEAT, HALF)
    theirs = scatter(meta, (1 - seq).reshape(1), own, other, back, bf16)
    received = lax.ppermute(theirs, "seq", [(0, 1), (1, 0)])
    mine = scatter(meta, seq.reshape(1), own, other, back, f32)
    return (out[None], mine + received.astype(f32))


def solution(mesh):
    in_specs = (P(None, "seq"), P(), P("col", None), P(), P(), P("col", "seq", None))
    out_specs = (P("col", "seq", None), P("col", "seq"))
    return jax.shard_map(
        per_device, mesh=mesh, in_specs=in_specs, out_specs=out_specs, check_vma=False
    )
```

time: 615 us -> 163 us (0.27)
  other arithmetic: 210 us -> 3.59 us
  local copies, waits for them, and re-layouts: 196 us -> 2.53 us
  Pallas kernels: 0 us -> 80.2 us
  waiting for transfers between devices: 78.9 us -> 20.7 us
  matrix products: 52.4 us -> 0 us
  blocking collectives: 53 us -> 32.3 us
    scatter-add x1 -> x0, other arithmetic: 187 us -> none  [per_device(): jnp.zeros((item_table.shape[1], feat_cols), jnp.float32).at[flat_items]]
    gather x2 -> x0, local copies, waits for them, and re-layouts: 123 us -> none  [per_device(): jnp.take(item_major, flat_items, axis=0).astype(jnp.bfloat16)]
    pallas_call x0 -> x4, Pallas kernels: none -> 80.2 us  [the longest x2 31.1 us: scatter(): pl.pallas_call(scatter_kernel, in_specs=[smem(), smem(), vmem(), vmem(),...]
    all_to_all x3 -> x1, waiting for transfers between devices: 78.9 us -> 19.2 us  [per_device(): back = lax.all_to_all(grad, both, split_axis=0, concat_axis=0, tiled=True)]
    dot_general x10 -> x0, matrix products: 52.4 us -> none  [the longest x1 11.6 us: per_device(): jnp.einsum('qhd,khd->hqk', attended_heads, values_in, preferred_element_t...]
    reshape x8 -> x1, local copies, waits for them, and re-layouts: 40.8 us -> 0.91 us  [per_device(): own = history_items.reshape(USERS * NBLK, BLK)]
    all_to_all x2 -> x1, blocking collectives: 53 us -> 32.3 us  [per_device(): lax.all_to_all(flat, both, split_axis=0, concat_axis=0, tiled=True)]
    unnamed x37 -> x6, local copies, waits for them, and re-layouts: 19 us -> 1.61 us
  transfers between devices with their start and end apart: 3 -> 3, of which waited for: 3 -> 2; matrix products, arithmetic and copies ran while one was open for 3% -> 1% of each run, Pallas kernels for 0% -> 10%
where the time goes in v1:
time: 163 us; the launch traced here: 161 us
  Pallas kernels  80.2 us (49%)
  blocking collectives  32.3 us (20%)
  starting transfers between devices  20.7 us (13%)
  waiting for transfers between devices  20.7 us (13%)
  other arithmetic  3.59 us (2%)
  local copies, waits for them, and re-layouts  2.53 us (2%)
    all_to_all x1, blocking collectives, per_device(): lax.all_to_all(flat, both, split_axis=0, concat_axis=0, tiled=True)  32.3 us
    pallas_call x2, Pallas kernels, scatter(): pl.pallas_call(scatter_kernel, in_specs=[smem(), smem(), vmem(), vmem(),...  31.1 us
    pallas_call x1, Pallas kernels, gather(): pl.pallas_call(gather_kernel, in_specs=[smem(), vmem(), vmem(), vmem()],...  27.8 us
    pallas_call x1, Pallas kernels, layer(): pl.pallas_call(layer_kernel, in_specs=[smem(), vmem(), vmem(), vmem(), vm...  21.3 us
    all_to_all x1, waiting for transfers between devices, per_device(): back = lax.all_to_all(grad, both, split_axis=0, concat_axis=0, tiled=True)  19.2 us
    all_to_all x1, starting transfers between devices, per_device(): back = lax.all_to_all(grad, both, split_axis=0, concat_axis=0, tiled=True)  17 us
  transfers between devices with their start and end apart: 3, of which 2 were waited for; matrix products, arithmetic and copies ran while one was open for 1% of the time, Pallas kernels for 10%

profile of v1, /device:TPU:1, one launch (start us, length us, event | category | flops | bytes accessed | tf_op | source)
XLA Modules:
  0.0 160.7 jit_solution(2575234089154688179)
XLA Ops:
  0.6 0.9 reshape.23.own_ref
  1.5 0.0 copy-start.1
  1.6 2.1 %collective-permute-start = (s32[256,128]{1,0:T(8,128)S(1)}, s32[256,128]{1,0:T(8,128)S(1)}, u32[]{:S(2)}, u32[]{:S(2)}) collective-permute-start(s32[256,128]{1,0:T(8,128)S(1)} %reshape.23.own_ref), channel_id=1, source_target_pairs={{0,1},{1,0},{2,3},{3,2},{4,5},{5,4},{6,7},{7,6},{8,9},{9,8},{10,11... | collective-permute-start | bytes 393224 | tf_op jit(solution)/shard_map/ppermute | solution.py:456
  3.7 1.3 pad_add_fusion.meta_ref
  5.0 1.5 collective-permute-done.other_ref
  6.4 0.0 copy-done.1
  6.5 0.0 copy-start.2
  6.5 0.6 copy-done.2
  7.1 27.8 %gather.1 = bf16[64,2,8,512]{3,2,1,0:T(8,128)(2,1)} custom-call(s32[66]{0:T(128)} %pad_add_fusion.meta_ref, s32[256,128]{1,0:T(8,128)} %copy-done.1, s32[256,128]{1,0:T(8,128)} %copy-done.2, f32[8,65536]{1,0:T(8,128)} %table_ref.1), custom_call_target="tpu_custom_call" | custom-call | tf_op jit(solution)/shard_map/gather/pallas_call | solution.py:385
  34.9 32.3 %all_to_all.10 = bf16[128,8,512]{2,1,0:T(8,128)(2,1)} all-to-all(bf16[128,8,512]{2,1,0:T(8,128)(2,1)} %bitcast.12), channel_id=1, replica_groups=mesh['col'=64,'seq'=2] {'col','seq'}, dimensions={0} | all-to-all | bytes 2097152 | tf_op jit(solution)/shard_map/all_to_all | solution.py:460
  67.2 21.3 %layer.1 = (bf16[512,512]{1,0:T(8,128)(2,1)}, bf16[64,2,8,512]{3,2,1,0:T(8,128)(2,1)}) custom-call(s32[66]{0:T(128)} %pad_add_fusion.meta_ref, bf16[64,2,8,512]{3,2,1,0:T(8,128)(2,1)} %bitcast.11, bf16[512,2048]{1,0:T(8,128)(2,1)} %w_ref.1, bf16[512,512]{1,0:T(8,128)(2,1)} %wo_ref.1, bf16[512,512]{1,0:T(8,128)(2,1)} %bitcast.14), custom_call_target="tpu_custom_call" | custom-call | tf_op jit(solution)/shard_map/layer/pallas_call | solution.py:417
  88.5 17.0 %all-to-all-start.1 = ((bf16[128,8,512]{2,1,0:T(8,128)(2,1)}), bf16[128,8,512]{2,1,0:T(8,128)(2,1)S(1)}, u32[]{:S(2)}, u32[]{:S(2)}) async-start(bf16[128,8,512]{2,1,0:T(8,128)(2,1)} %bitcast.13), calls=%async_computation.1 | async-start | bytes 2097152 | tf_op jit(solution)/shard_map/all_to_all | solution.py:464
  105.5 19.2 %all-to-all-done.1 = bf16[128,8,512]{2,1,0:T(8,128)(2,1)S(1)} async-done(((bf16[128,8,512]{2,1,0:T(8,128)(2,1)}), bf16[128,8,512]{2,1,0:T(8,128)(2,1)S(1)}, u32[]{:S(2)}, u32[]{:S(2)}) %all-to-all-start.1) | async-done | bytes 1048608 | tf_op jit(solution)/shard_map/all_to_all | solution.py:464
  124.7 0.0 copy-start
  124.7 1.0 copy-done
  125.7 15.5 %scatter.3 = bf16[8,32768]{1,0:T(8,128)(2,1)} custom-call(s32[66]{0:T(128)} %pad_add_fusion.meta_ref, s32[1]{0:T(128)} %bitcast.8.half_ref, s32[256,128]{1,0:T(8,128)} %copy-done.1, s32[256,128]{1,0:T(8,128)} %copy-done.2, bf16[64,2,8,512]{3,2,1,0:T(8,128)(2,1)} %bitcast.9), custom_call_target="tpu_custom_call" | custom-call | tf_op jit(solution)/shard_map/scatter/pallas_call | solution.py:401
  141.2 1.6 %collective-permute-start.1 = (bf16[8,32768]{1,0:T(8,128)(2,1)}, bf16[8,32768]{1,0:T(8,128)(2,1)S(1)}, u32[]{:S(2)}, u32[]{:S(2)}) collective-permute-start(bf16[8,32768]{1,0:T(8,128)(2,1)} %scatter.3), channel_id=1, source_target_pairs={{0,1},{1,0},{2,3},{3,2},{4,5},{5,4},{6,7},{7,6},{8,9},{9,8},{10,11... | collective-permute-start | bytes 1572872 | tf_op jit(solution)/shard_map/ppermute | solution.py:467
  142.8 15.6 %scatter.2 = f32[8,32768]{1,0:T(8,128)} custom-call(s32[66]{0:T(128)} %pad_add_fusion.meta_ref, s32[1]{0:T(128)} %bitcast.half_ref, s32[256,128]{1,0:T(8,128)} %copy-done.1, s32[256,128]{1,0:T(8,128)} %copy-done.2, bf16[64,2,8,512]{3,2,1,0:T(8,128)(2,1)} %bitcast.10), custom_call_target="tpu_custom_call" | custom-call | tf_op jit(solution)/shard_map/scatter/pallas_call | solution.py:401
  158.4 0.0 collective-permute-done.1
  158.4 2.3 %convert_add_fusion = f32[8,32768]{1,0:T(8,128)} fusion(f32[8,32768]{1,0:T(8,128)} %scatter.2, bf16[8,32768]{1,0:T(8,128)(2,1)S(1)} %collective-permute-done.1), kind=kLoop, calls=%fused_computation | loop fusion | flops 524288 | bytes 2621440 | tf_op jit(solution)/shard_map/add | solution.py:469
Async XLA Ops:
  1.5 4.9 %copy-start.1 = (s32[256,128]{1,0:T(8,128)}, s32[256,128]{1,0:T(8,128)S(1)}, u32[]{:S(2)}) copy-start(s32[256,128]{1,0:T(8,128)S(1)} %reshape.23.own_ref) | copy-start | bytes 393220
  1.6 4.9 %collective-permute-start = (s32[256,128]{1,0:T(8,128)S(1)}, s32[256,128]{1,0:T(8,128)S(1)}, u32[]{:S(2)}, u32[]{:S(2)}) collective-permute-start(s32[256,128]{1,0:T(8,128)S(1)} %reshape.23.own_ref), channel_id=1, source_target_pairs={{0,1},{1,0},{2,3},{3,2},{4,5},{5,4},{6,7},{7,6},{8,9},{9,8},{10,11... | collective-permute-start | bytes 393224 | tf_op jit(solution)/shard_map/ppermute | solution.py:456
  6.5 0.6 copy-start.2
  88.5 36.2 %all-to-all-start.1 = ((bf16[128,8,512]{2,1,0:T(8,128)(2,1)}), bf16[128,8,512]{2,1,0:T(8,128)(2,1)S(1)}, u32[]{:S(2)}, u32[]{:S(2)}) async-start(bf16[128,8,512]{2,1,0:T(8,128)(2,1)} %bitcast.13), calls=%async_computation.1 | async-start | bytes 2097152 | tf_op jit(solution)/shard_map/all_to_all | solution.py:464
  124.7 1.0 copy-start
  141.2 17.3 %collective-permute-start.1 = (bf16[8,32768]{1,0:T(8,128)(2,1)}, bf16[8,32768]{1,0:T(8,128)(2,1)S(1)}, u32[]{:S(2)}, u32[]{:S(2)}) collective-permute-start(bf16[8,32768]{1,0:T(8,128)(2,1)} %scatter.3), channel_id=1, source_target_pairs={{0,1},{1,0},{2,3},{3,2},{4,5},{5,4},{6,7},{7,6},{8,9},{9,8},{10,11... | collective-permute-start | bytes 1572872 | tf_op jit(solution)/shard_map/ppermute | solution.py:467

commit v2 on v1

--- a/solution.py
+++ b/solution.py
@@ -21,7 +21,7 @@
 bf16 = jnp.bfloat16
 f32 = jnp.float32
 
-G_LO = 32
+G_LO = 16
 G_HI = ROWS // G_LO
 G_STEP = 8
 S_ROWS = ROWS // 2
@@ -30,12 +30,10 @@
 S_STEP = 16
 
 
-def block_list(meta_ref, list_ref):
-    seq = meta_ref[0]
-
+def block_list(seq, lengths_ref, list_ref):
     def step(u, count):
         parity = (seq + u) & 1
-        blocks = (meta_ref[2 + u] + (BLK - 1)) // BLK
+        blocks = (lengths_ref[u] + (BLK - 1)) // BLK
         for i in range(NBLK):
             list_ref[count + i] = u * NBLK + i
         return count + (blocks + 1 - parity) // 2
@@ -47,15 +45,13 @@
     u = block // NBLK
     i = block % NBLK
     parity = (seq + u) & 1
-    half = i // 2
-    row = half * (USERS * NBLK) + u * NBLK + 2 * (i % 2) + parity
-    return items_ref[pl.ds(row, 1), :]
+    return items_ref[i // 2, 2 * (i % 2) + parity, pl.ds(u, 1), :]
 
 
 def stage_items(seq, own_ref, other_ref, items_ref):
-    n = USERS * NBLK
-    items_ref[pl.ds(pl.multiple_of(seq * n, n), n), :] = own_ref[...]
-    items_ref[pl.ds(pl.multiple_of((1 - seq) * n, n), n), :] = other_ref[...]
+    for b in range(NBLK):
+        items_ref[seq, b] = own_ref[:, b * BLK : (b + 1) * BLK]
+        items_ref[1 - seq, b] = other_ref[:, b * BLK : (b + 1) * BLK]
 
 
 def onehot(index, rows):
@@ -65,44 +61,82 @@
     return jnp.where(iota == wide, jnp.ones((), bf16), jnp.zeros((), bf16))
 
 
-def gather_kernel(meta_ref, own_ref, other_ref, table_ref, out_ref, t_ref, items_ref, list_ref):
-    seq = meta_ref[0]
+def rows_kernel(table_ref, rows_ref):
+    step = 512
+    for c in range(G_HI // step):
+        parts = [
+            table_ref[:, lo * G_HI + c * step : lo * G_HI + (c + 1) * step] for lo in range(G_LO)
+        ]
+        rows_ref[c * step : (c + 1) * step, :] = jnp.concatenate(parts, axis=0).T
+
+
+def gather_kernel(
+    seq_ref, lengths_ref, own_ref, other_ref, rows_ref, out_ref,
+    items_ref, stage_ref, got_ref, list_ref, index_ref, sems,
+):
+    seq = seq_ref[0]
     stage_items(seq, own_ref, other_ref, items_ref)
-    for lo in range(G_LO):
-        t_ref[lo * FEAT : (lo + 1) * FEAT, :] = table_ref[:, lo * G_HI : (lo + 1) * G_HI].astype(bf16)
     out_ref[...] = jnp.zeros_like(out_ref)
-    count = block_list(meta_ref, list_ref)
-
-    def step(g, carry):
-        ids = []
+    count = block_list(seq, lengths_ref, list_ref)
+    pairs = (count + 2 * G_STEP - 1) // (2 * G_STEP)
+
+    def ids_of(g):
+        last = count - 1
+        return [list_ref[jnp.minimum(g * G_STEP + j, last)] for j in range(G_STEP)]
+
+    def copy(slot):
+        return pltpu.make_async_copy(stage_ref.at[slot], index_ref.at[slot], sems.at[slot])
+
+    def fetch(g, slot):
+        rows = jnp.concatenate([item_row(items_ref, seq, b) for b in ids_of(g)], axis=0)
+        stage_ref[slot] = rows & (G_HI - 1)
+        copy(slot).start()
+
+    def move(slot):
         for j in range(G_STEP):
-            b = jnp.minimum(g * G_STEP + j, count - 1)
-            ids.append(list_ref[jnp.maximum(b, 0)])
-        index = jnp.concatenate([item_row(items_ref, seq, b) for b in ids], axis=1)
-        lo = lax.shift_right_logical(index, 11)
-        hi = index & (G_HI - 1)
-        acc = jnp.dot(t_ref[...], onehot(hi, G_HI), preferred_element_type=f32)
-        n = G_STEP * BLK
-        acc = acc.reshape(G_LO, FEAT, n)
-        mask = lax.broadcasted_iota(jnp.int32, (G_LO, FEAT, n), 0) == lo.reshape(1, 1, n)
-        picked = jnp.sum(jnp.where(mask, acc, 0.0), axis=0).astype(bf16)
+            for t in range(BLK):
+                r = index_ref[slot, j, t]
+                got_ref[slot, pl.ds(j * BLK + t, 1), :] = rows_ref[pl.ds(r, 1), :]
+
+    def finish(g, slot):
+        ids = ids_of(g)
         for j in range(G_STEP):
             u = ids[j] // NBLK
             col = pl.multiple_of((ids[j] % NBLK) * BLK, BLK)
-            part = picked[:, j * BLK : (j + 1) * BLK]
+            lo = lax.shift_right_logical(item_row(items_ref, seq, ids[j]), 12)
+            part = got_ref[slot, j * BLK : (j + 1) * BLK, :].T.reshape(G_LO, FEAT, BLK)
+            mask = lax.broadcasted_iota(jnp.int32, (G_LO, FEAT, BLK), 0) == lo.reshape(1, 1, BLK)
+            part = jnp.sum(jnp.where(mask, part, 0.0), axis=0).astype(bf16)
             out_ref[u, 0, :, pl.ds(col, BLK)] = part
             out_ref[u, 1, :, pl.ds(col, BLK)] = part
+
+    got_ref[1] = jnp.zeros_like(got_ref[1])
+    for slot in range(2):
+        fetch(slot, slot)
+
+    def step(p, carry):
+        for slot in range(2):
+            g = 2 * p + slot
+            copy(slot).wait()
+            move(slot)
+            finish(jnp.maximum(g - 1, 0), 1 - slot)
+            fetch(g + 2, slot)
         return carry
 
-    lax.fori_loop(0, (count + G_STEP - 1) // G_STEP, step, 0)
-
-
-def scatter_kernel(meta_ref, half_ref, own_ref, other_ref, grad_ref, out_ref, items_ref, acc_ref, list_ref):
-    seq = meta_ref[0]
+    lax.fori_loop(0, pairs, step, 0)
+    finish(2 * pairs - 1, 1)
+    for slot in range(2):
+        copy(slot).wait()
+
+
+def scatter_kernel(
+    seq_ref, lengths_ref, half_ref, own_ref, other_ref, grad_ref, out_ref, items_ref, acc_ref, list_ref
+):
+    seq = seq_ref[0]
     base = half_ref[0] * S_ROWS
     stage_items(seq, own_ref, other_ref, items_ref)
     acc_ref[...] = jnp.zeros_like(acc_ref)
-    count = block_list(meta_ref, list_ref)
+    count = block_list(seq, lengths_ref, list_ref)
 
     def step(g, carry):
         rows, grads = [], []
@@ -168,13 +202,13 @@
 
 
 def layer_kernel(
-    meta_ref, e_ref, w_ref, wo_ref, cot_ref, out_ref, g_ref,
+    seq_ref, col_ref, lengths_ref, e_ref, w_ref, wo_ref, cot_ref, out_ref, g_ref,
     x_ref, y_ref, r_ref, yl_ref, rl_ref, slope_ref, slopel_ref, u_ref, q_ref, k_ref, v_ref,
     p_ref, d_ref, pl_ref, dl_ref, att_ref, do_ref, pg_ref, pgl_ref,
 ):
-    seq = meta_ref[0]
-    col = meta_ref[1]
-    length = meta_ref[2 + col]
+    seq = seq_ref[0]
+    col = col_ref[0]
+    length = lengths_ref[col]
     base = seq * HALF
     upper = seq == 1
     active = length > base
@@ -381,42 +415,56 @@
     return pltpu.CompilerParams(vmem_limit_bytes=60 * 1024 * 1024)
 
 
-def gather(meta, own, other, table):
+def table_rows(table):
+    return pl.pallas_call(
+        rows_kernel,
+        in_specs=[vmem()],
+        out_specs=vmem(),
+        out_shape=jax.ShapeDtypeStruct((G_HI, BLK), f32),
+        compiler_params=params(),
+        name="table_rows",
+    )(table)
+
+
+def gather(seq, lengths, own, other, rows):
     return pl.pallas_call(
         gather_kernel,
-        in_specs=[smem(), vmem(), vmem(), vmem()],
+        in_specs=[smem(), smem(), vmem(), vmem(), vmem()],
         out_specs=vmem(),
         out_shape=jax.ShapeDtypeStruct((USERS, 2, FEAT, HALF), bf16),
         scratch_shapes=[
-            pltpu.VMEM((G_LO * FEAT, G_HI), bf16),
-            pltpu.VMEM((2 * USERS * NBLK, BLK), jnp.int32),
+            pltpu.VMEM((2, NBLK, USERS, BLK), jnp.int32),
+            pltpu.VMEM((2, G_STEP, BLK), jnp.int32),
+            pltpu.VMEM((2, G_STEP * BLK, BLK), f32),
             pltpu.SMEM((USERS * NBLK + NBLK,), jnp.int32),
+            pltpu.SMEM((2, G_STEP, BLK), jnp.int32),
+            pltpu.SemaphoreType.DMA((2,)),
         ],
         compiler_params=params(),
         name="gather",
-    )(meta, own, other, table)
-
-
-def scatter(meta, half, own, other, grad, dtype):
+    )(seq, lengths, own, other, rows)
+
+
+def scatter(seq, lengths, half, own, other, grad, dtype):
     return pl.pallas_call(
         scatter_kernel,
-        in_specs=[smem(), smem(), vmem(), vmem(), vmem()],
+        in_specs=[smem(), smem(), smem(), vmem(), vmem(), vmem()],
         out_specs=vmem(),
         out_shape=jax.ShapeDtypeStruct((FEAT, S_ROWS), dtype),
         scratch_shapes=[
-            pltpu.VMEM((2 * USERS * NBLK, BLK), jnp.int32),
+            pltpu.VMEM((2, NBLK, USERS, BLK), jnp.int32),
             pltpu.VMEM((S_LO * FEAT, S_HI), f32),
             pltpu.SMEM((USERS * NBLK + NBLK,), jnp.int32),
         ],
         compiler_params=params(),
         name="scatter",
-    )(meta, half, own, other, grad)
-
-
-def layer(meta, e, w, wo, cot):
+    )(seq, lengths, half, own, other, grad)
+
+
+def layer(seq, col, lengths, e, w, wo, cot):
     return pl.pallas_call(
         layer_kernel,
-        in_specs=[smem(), vmem(), vmem(), vmem(), vmem()],
+        in_specs=[smem(), smem(), smem(), vmem(), vmem(), vmem(), vmem()],
         out_specs=(vmem(), vmem()),
         out_shape=(
             jax.ShapeDtypeStruct((HALF, D), bf16),
@@ -445,27 +493,30 @@
         ],
         compiler_params=params(),
         name="layer",
-    )(meta, e, w, wo, cot)
+    )(seq, col, lengths, e, w, wo, cot)
 
 
 def per_device(history_items, lengths, item_table, input_weight, output_weight, output_cotangent):
-    col = lax.axis_index("col").astype(jnp.int32)
-    seq = lax.axis_index("seq").astype(jnp.int32)
-    meta = jnp.concatenate([jnp.stack([seq, col]), lengths])
-    own = history_items.reshape(USERS * NBLK, BLK)
-    other = lax.ppermute(own, "seq", [(0, 1), (1, 0)])
-    looked = gather(meta, own, other, item_table)
+    col = lax.axis_index("col").astype(jnp.int32).reshape(1)
+    seq = lax.axis_index("seq").astype(jnp.int32).reshape(1)
+    swap = [(0, 1), (1, 0)]
     both = ("col", "seq")
+    own = history_items
+    other = lax.ppermute(own, "seq", swap)
+    rows = table_rows(item_table)
+    looked = gather(seq, lengths, own, other, rows)
     flat = looked.reshape(2 * USERS, FEAT, HALF)
     arrived = lax.all_to_all(flat, both, split_axis=0, concat_axis=0, tiled=True)
     arrived = arrived.reshape(USERS, 2, FEAT, HALF)
-    out, grad = layer(meta, arrived, input_weight, output_weight, output_cotangent[0])
+    out, grad = layer(
+        seq, col, lengths, arrived, input_weight, output_weight, output_cotangent[0]
+    )
     grad = grad.reshape(2 * USERS, FEAT, HALF)
     back = lax.all_to_all(grad, both, split_axis=0, concat_axis=0, tiled=True)
     back = back.reshape(USERS, 2, FEAT, HALF)
-    theirs = scatter(meta, (1 - seq).reshape(1), own, other, back, bf16)
-    received = lax.ppermute(theirs, "seq", [(0, 1), (1, 0)])
-    mine = scatter(meta, seq.reshape(1), own, other, back, f32)
+    theirs = scatter(seq, lengths, 1 - seq, own, other, back, bf16)
+    received = lax.ppermute(theirs, "seq", swap)
+    mine = scatter(seq, lengths, seq, own, other, back, f32)
     return (out[None], mine + received.astype(f32))
 
 

time: 163 us -> 157 us (0.963)
  blocking collectives: 32.3 us -> 0 us
  waiting for transfers between devices: 20.7 us -> 38.4 us
  starting transfers between devices: 20.7 us -> 30.7 us
    all_to_all x1 -> x0, blocking collectives: 32.3 us -> none  [per_device(): lax.all_to_all(flat, both, split_axis=0, concat_axis=0, tiled=True)]
    all_to_all x0 -> x1, waiting for transfers between devices: none -> 19.2 us  [per_device(): lax.all_to_all(flat, both, split_axis=0, concat_axis=0, tiled=True)]
    all_to_all x0 -> x1, starting transfers between devices: none -> 11.4 us  [per_device(): lax.all_to_all(flat, both, split_axis=0, concat_axis=0, tiled=True)]
    pallas_call x4 -> x5, Pallas kernels: 80.2 us -> 80.1 us  [the longest x2 33.6 us: scatter(): pl.pallas_call(scatter_kernel, in_specs=[smem(), smem(), smem(), vmem(),...]
  transfers between devices with their start and end apart: 3 -> 4, of which waited for: 2 -> 2; matrix products, arithmetic and copies ran while one was open for 1% -> 0% of each run, Pallas kernels for 10% -> 13%
where the time goes in v2:
time: 157 us; the launch traced here: 155 us
  Pallas kernels  80.1 us (51%)
  waiting for transfers between devices  38.4 us (24%)
  starting transfers between devices  30.7 us (20%)
  local copies, waits for them, and re-layouts  2.59 us (2%)
  other arithmetic  2.28 us (1%)
    pallas_call x2, Pallas kernels, scatter(): pl.pallas_call(scatter_kernel, in_specs=[smem(), smem(), smem(), vmem(),...  33.6 us
    pallas_call x1, Pallas kernels, gather(): pl.pallas_call(gather_kernel, in_specs=[smem(), smem(), vmem(), vmem(), v...  21.7 us
    pallas_call x1, Pallas kernels, layer(): pl.pallas_call(layer_kernel, in_specs=[smem(), smem(), smem(), vmem(), vm...  21.3 us
    all_to_all x1, waiting for transfers between devices, per_device(): back = lax.all_to_all(grad, both, split_axis=0, concat_axis=0, tiled=True)  19.2 us
    all_to_all x1, waiting for transfers between devices, per_device(): lax.all_to_all(flat, both, split_axis=0, concat_axis=0, tiled=True)  19.2 us
    all_to_all x1, starting transfers between devices, per_device(): back = lax.all_to_all(grad, both, split_axis=0, concat_axis=0, tiled=True)  17 us
    all_to_all x1, starting transfers between devices, per_device(): lax.all_to_all(flat, both, split_axis=0, concat_axis=0, tiled=True)  11.4 us
    pallas_call x1, Pallas kernels, table_rows(): pl.pallas_call(rows_kernel, in_specs=[vmem()], out_specs=vmem(), out_shap...  3.53 us
  transfers between devices with their start and end apart: 4, of which 2 were waited for; matrix products, arithmetic and copies ran while one was open for 0% of the time, Pallas kernels for 13%

profile of v2, /device:TPU:1, one launch (start us, length us, event | category | flops | bytes accessed | tf_op | source)
XLA Modules:
  0.0 154.8 jit_solution(3012099563451936545)
XLA Ops:
  0.6 2.1 %collective-permute-start = (s32[64,512]{1,0:T(8,128)}, s32[64,512]{1,0:T(8,128)S(1)}, u32[]{:S(2)}, u32[]{:S(2)}) collective-permute-start(s32[64,512]{1,0:T(8,128)} %own_ref.5), channel_id=1, source_target_pairs={{0,1},{1,0},{2,3},{3,2},{4,5},{5,4},{6,7},{7,6},{8,9},{9,8},{10,11... | collective-permute-start | bytes 393224 | tf_op jit(solution)/shard_map/ppermute | solution.py:505
  2.7 3.5 %table_rows.1.rows_ref = f32[4096,128]{1,0:T(8,128)} custom-call(f32[8,65536]{1,0:T(8,128)} %table_ref.1), custom_call_target="tpu_custom_call" | custom-call | tf_op jit(solution)/shard_map/table_rows/pallas_call | solution.py:419
  6.3 0.0 collective-permute-done.other_ref
  6.3 0.0 copy-start.2
  6.3 0.7 copy-done.2
  6.9 21.7 %gather.1 = bf16[64,2,8,512]{3,2,1,0:T(8,128)(2,1)} custom-call(s32[1]{0:T(128)} %bitcast.seq_ref.half_ref, s32[64]{0:T(128)} %lengths_ref.7, s32[64,512]{1,0:T(8,128)} %own_ref.5, s32[64,512]{1,0:T(8,128)} %copy-done.2, f32[4096,128]{1,0:T(8,128)} %table_rows.1.rows_ref), custom_call_target="tpu_custom_call" | custom-call | tf_op jit(solution)/shard_map/gather/pallas_call | solution.py:430
  28.6 11.4 %all-to-all-start = ((bf16[128,8,512]{2,1,0:T(8,128)(2,1)}), bf16[128,8,512]{2,1,0:T(8,128)(2,1)S(1)}, u32[]{:S(2)}, u32[]{:S(2)}) async-start(bf16[128,8,512]{2,1,0:T(8,128)(2,1)} %bitcast.11), calls=%async_computation | async-start | bytes 2097152 | tf_op jit(solution)/shard_map/all_to_all | solution.py:509
  40.0 19.2 %all-to-all-done = bf16[128,8,512]{2,1,0:T(8,128)(2,1)S(1)} async-done(((bf16[128,8,512]{2,1,0:T(8,128)(2,1)}), bf16[128,8,512]{2,1,0:T(8,128)(2,1)S(1)}, u32[]{:S(2)}, u32[]{:S(2)}) %all-to-all-start) | async-done | bytes 1048608 | tf_op jit(solution)/shard_map/all_to_all | solution.py:509
  59.2 0.0 copy-start.1
  59.2 1.0 copy-done.1
  60.2 21.3 %layer.1 = (bf16[512,512]{1,0:T(8,128)(2,1)}, bf16[64,2,8,512]{3,2,1,0:T(8,128)(2,1)}) custom-call(s32[1]{0:T(128)} %bitcast.seq_ref.half_ref, s32[1]{0:T(128)} %bitcast.1.col_ref, s32[64]{0:T(128)} %lengths_ref.7, bf16[64,2,8,512]{3,2,1,0:T(8,128)(2,1)} %bitcast.10, bf16[512,2048]{1,0:T(8,128)(2,1)} %w_ref.1, bf16[512,512]{1,0:T(8,128)(2,1)} %wo_ref.1, ...), custom_call_target="tpu_custom_call" | custom-call | tf_op jit(solution)/shard_map/layer/pallas_call | solution.py:465
  81.5 17.0 %all-to-all-start.1 = ((bf16[128,8,512]{2,1,0:T(8,128)(2,1)}), bf16[128,8,512]{2,1,0:T(8,128)(2,1)S(1)}, u32[]{:S(2)}, u32[]{:S(2)}) async-start(bf16[128,8,512]{2,1,0:T(8,128)(2,1)} %bitcast.12), calls=%async_computation.1 | async-start | bytes 2097152 | tf_op jit(solution)/shard_map/all_to_all | solution.py:515
  98.4 19.2 %all-to-all-done.1 = bf16[128,8,512]{2,1,0:T(8,128)(2,1)S(1)} async-done(((bf16[128,8,512]{2,1,0:T(8,128)(2,1)}), bf16[128,8,512]{2,1,0:T(8,128)(2,1)S(1)}, u32[]{:S(2)}, u32[]{:S(2)}) %all-to-all-start.1) | async-done | bytes 1048608 | tf_op jit(solution)/shard_map/all_to_all | solution.py:515
  117.7 0.0 copy-start
  117.7 1.0 copy-done
  118.6 16.7 %scatter.3 = bf16[8,32768]{1,0:T(8,128)(2,1)} custom-call(s32[1]{0:T(128)} %bitcast.seq_ref.half_ref, s32[64]{0:T(128)} %lengths_ref.7, s32[1]{0:T(128)S(6)} %sub.3.half_ref, s32[64,512]{1,0:T(8,128)} %own_ref.5, s32[64,512]{1,0:T(8,128)} %copy-done.2, bf16[64,2,8,512]{3,2,1,0:T(8,128)(2,1)} %bitcast.8), custom_call_target="tpu_custom_call" | custom-call | tf_op jit(solution)/shard_map/scatter/pallas_call | solution.py:449
  135.4 0.3 collective-permute-start.1
  135.6 16.9 %scatter.2 = f32[8,32768]{1,0:T(8,128)} custom-call(s32[1]{0:T(128)} %bitcast.seq_ref.half_ref, s32[64]{0:T(128)} %lengths_ref.7, s32[1]{0:T(128)} %bitcast.seq_ref.half_ref, s32[64,512]{1,0:T(8,128)} %own_ref.5, s32[64,512]{1,0:T(8,128)} %copy-done.2, bf16[64,2,8,512]{3,2,1,0:T(8,128)(2,1)} %bitcast.9), custom_call_target="tpu_custom_call" | custom-call | tf_op jit(solution)/shard_map/scatter/pallas_call | solution.py:449
  152.5 0.0 collective-permute-done.1
  152.5 2.3 %convert_add_fusion = f32[8,32768]{1,0:T(8,128)} fusion(f32[8,32768]{1,0:T(8,128)} %scatter.2, bf16[8,32768]{1,0:T(8,128)(2,1)S(1)} %collective-permute-done.1), kind=kLoop, calls=%fused_computation | loop fusion | flops 524288 | bytes 2621440 | tf_op jit(solution)/shard_map/add | solution.py:520
Async XLA Ops:
  0.6 5.6 %collective-permute-start = (s32[64,512]{1,0:T(8,128)}, s32[64,512]{1,0:T(8,128)S(1)}, u32[]{:S(2)}, u32[]{:S(2)}) collective-permute-start(s32[64,512]{1,0:T(8,128)} %own_ref.5), channel_id=1, source_target_pairs={{0,1},{1,0},{2,3},{3,2},{4,5},{5,4},{6,7},{7,6},{8,9},{9,8},{10,11... | collective-permute-start | bytes 393224 | tf_op jit(solution)/shard_map/ppermute | solution.py:505
  6.3 0.7 copy-start.2
  28.6 30.6 %all-to-all-start = ((bf16[128,8,512]{2,1,0:T(8,128)(2,1)}), bf16[128,8,512]{2,1,0:T(8,128)(2,1)S(1)}, u32[]{:S(2)}, u32[]{:S(2)}) async-start(bf16[128,8,512]{2,1,0:T(8,128)(2,1)} %bitcast.11), calls=%async_computation | async-start | bytes 2097152 | tf_op jit(solution)/shard_map/all_to_all | solution.py:509
  59.2 1.0 copy-start.1
  81.5 36.2 %all-to-all-start.1 = ((bf16[128,8,512]{2,1,0:T(8,128)(2,1)}), bf16[128,8,512]{2,1,0:T(8,128)(2,1)S(1)}, u32[]{:S(2)}, u32[]{:S(2)}) async-start(bf16[128,8,512]{2,1,0:T(8,128)(2,1)} %bitcast.12), calls=%async_computation.1 | async-start | bytes 2097152 | tf_op jit(solution)/shard_map/all_to_all | solution.py:515
  117.7 1.0 copy-start
  135.4 17.2 %collective-permute-start.1 = (bf16[8,32768]{1,0:T(8,128)(2,1)}, bf16[8,32768]{1,0:T(8,128)(2,1)S(1)}, u32[]{:S(2)}, u32[]{:S(2)}) collective-permute-start(bf16[8,32768]{1,0:T(8,128)(2,1)} %scatter.3), channel_id=1, source_target_pairs={{0,1},{1,0},{2,3},{3,2},{4,5},{5,4},{6,7},{7,6},{8,9},{9,8},{10,11... | collective-permute-start | bytes 1572872 | tf_op jit(solution)/shard_map/ppermute | solution.py:518

commit v3 on v2

--- a/solution.py
+++ b/solution.py
@@ -175,10 +175,6 @@
     return lax.dot_general(a, b, (((1,), (1,)), ((), ())), preferred_element_type=f32)
 
 
-def dot_tn(a, b):
-    return lax.dot_general(a, b, (((0,), (0,)), ((), ())), preferred_element_type=f32)
-
-
 def dot_nn(a, b):
     return jnp.dot(a, b, preferred_element_type=f32)
 
@@ -197,14 +193,18 @@
     return r * (dy - a - y * b)
 
 
-def sigmoid(x):
-    return 0.5 * jnp.tanh(0.5 * x) + 0.5
+def gate(h):
+    t = jnp.tanh(h)
+    a = 1.0 + t
+    act = h * a
+    return act, a + act * (1.0 - t)
 
 
 def layer_kernel(
     seq_ref, col_ref, lengths_ref, e_ref, w_ref, wo_ref, cot_ref, out_ref, g_ref,
-    x_ref, y_ref, r_ref, yl_ref, rl_ref, slope_ref, slopel_ref, u_ref, q_ref, k_ref, v_ref,
-    p_ref, d_ref, pl_ref, dl_ref, att_ref, do_ref, pg_ref, pgl_ref,
+    x_ref, y_ref, r_ref, yl_ref, rl_ref, slope_ref, slopel_ref, u_ref, q_ref, qt_ref, k_ref, kt_ref, v_ref, vt_ref,
+    p_ref, d_ref, pl_ref, dl_ref, att_ref, do_ref, dot_ref, dk_ref, dv_ref, dkl_ref, dvl_ref,
+    pg_ref, pgl_ref,
 ):
     seq = seq_ref[0]
     col = col_ref[0]
@@ -214,6 +214,8 @@
     active = length > base
     lanes = lax.broadcasted_iota(jnp.int32, (1, 2 * DH), 1)
     head_mask = [(lanes < DH).astype(f32).astype(bf16), (lanes >= DH).astype(f32).astype(bf16)]
+    QB = HALF // 2
+    parts = [slice(0, QB), slice(QB, HALF)]
 
     def place(half, b):
         i = 2 * half + b // 2
@@ -233,10 +235,110 @@
             dst, at = place(half, b)
             g_ref[:, dst, :, pl.ds(at, BLK)] = flat[:, :, b * BLK : (b + 1) * BLK]
 
-    def activate(pre):
-        s = sigmoid(pre)
-        act = pre * s
-        return act, s + act * (1.0 - s)
+    def pairs_of(act):
+        return [act[:, hp * 2 * DH : (hp + 1) * 2 * DH] for hp in range(PAIRS)]
+
+    def project(half, blocks, yb, slopes):
+        for n, blk in enumerate(blocks):
+            act, slope = gate(dot_nn(yb, w_ref[:, blk * HID : (blk + 1) * HID]))
+            slopes[:, n * HID : (n + 1) * HID] = slope
+            act = act.astype(bf16)
+            if blk == 0:
+                u_ref[...] = act
+            elif blk == 2:
+                act = act.astype(f32) * (0.5 * DH**-0.5)
+                qt_ref[...] = act.T.astype(bf16)
+                for hp, part in enumerate(pairs_of(act.astype(bf16))):
+                    q_ref[hp] = part
+            else:
+                target, turned = (v_ref, vt_ref) if blk == 1 else (k_ref, kt_ref)
+                turned[half] = act.T
+                for hp, part in enumerate(pairs_of(act)):
+                    target[half, hp] = part
+
+    def plus(a, b):
+        return b if a is None else a + b
+
+    def forward(hp, lower):
+        q, k = q_ref[hp], k_ref[1, hp]
+        if lower:
+            kl = k_ref[0, hp]
+        row = lax.broadcasted_iota(jnp.int32, (QB, 1), 0)
+        for h in range(2):
+            head = 2 * hp + h
+            hs = pl.ds(pl.multiple_of(head * DH, DH), DH)
+            vt = vt_ref[1, hs, :]
+            qm = q * head_mask[h]
+            att = [None, None]
+            for qi in range(2):
+                for ki in range(qi + 1):
+                    act, slope = gate(dot_nt(qm[parts[qi]], k[parts[ki]]))
+                    if ki == qi:
+                        limit = jnp.minimum(row, length - 1 - base - ki * QB)
+                        ok = lax.broadcasted_iota(jnp.int32, act.shape, 1) <= limit
+                        act = jnp.where(ok, act, 0.0)
+                        slope = jnp.where(ok, slope, 0.0)
+                    at = 2 * qi + ki
+                    p = act.astype(bf16)
+                    p_ref[head, at] = p
+                    d_ref[head, at] = slope
+                    att[qi] = plus(att[qi], dot_nt(vt[:, parts[ki]], p))
+                if lower:
+                    act, slope = gate(dot_nt(qm[parts[qi]], kl))
+                    p = act.astype(bf16)
+                    pl_ref[head, parts[qi]] = p
+                    dl_ref[head, parts[qi]] = slope
+                    att[qi] = att[qi] + dot_nt(vt_ref[0, hs, :], p)
+            att_ref[hs, :] = jnp.concatenate(att, axis=1)
+
+    def backward(hp, lower):
+        v, do = v_ref[1, hp], do_ref[hp]
+        if lower:
+            vl = v_ref[0, hp]
+        for h in range(2):
+            head = 2 * hp + h
+            hs = pl.ds(pl.multiple_of(head * DH, DH), DH)
+            qt = qt_ref[hs, :]
+            dot = dot_ref[hs, :]
+            kt = kt_ref[1, hs, :]
+            dm = do * head_mask[h]
+            dq = [None, None]
+            dk = [None, None]
+            dv = [None, None]
+            if lower:
+                dkl, dvl = None, None
+            for qi in range(2):
+                qs = parts[qi]
+                for ki in range(qi + 1):
+                    at = 2 * qi + ki
+                    ds = (dot_nt(dm[qs], v[parts[ki]]) * d_ref[head, at]).astype(bf16)
+                    dq[qi] = plus(dq[qi], dot_nt(kt[:, parts[ki]], ds))
+                    dk[ki] = plus(dk[ki], dot_nn(qt[:, qs], ds))
+                    dv[ki] = plus(dv[ki], dot_nn(dot[:, qs], p_ref[head, at]))
+                if lower:
+                    ds = (dot_nt(dm[qs], vl) * dl_ref[head, qs]).astype(bf16)
+                    dq[qi] = plus(dq[qi], dot_nt(kt_ref[0, hs, :], ds))
+                    dkl = plus(dkl, dot_nn(qt[:, qs], ds))
+                    dvl = plus(dvl, dot_nn(dot[:, qs], pl_ref[head, qs]))
+            att_ref[hs, :] = jnp.concatenate(dq, axis=1)
+            dk_ref[hs, :] = jnp.concatenate(dk, axis=1)
+            dv_ref[hs, :] = jnp.concatenate(dv, axis=1)
+            if lower:
+                dkl_ref[hs, :] = dkl
+                dvl_ref[hs, :] = dvl
+
+    def over_pairs(body):
+        @pl.when(upper)
+        def _():
+            @pl.loop(0, PAIRS)
+            def _(hp):
+                body(hp, True)
+
+        @pl.when(jnp.logical_not(upper))
+        def _():
+            @pl.loop(0, PAIRS)
+            def _(hp):
+                body(hp, False)
 
     g_ref[...] = jnp.zeros_like(g_ref)
 
@@ -250,89 +352,19 @@
         x_ref[...] = x
         y, r = norm(x)
         y_ref[...] = y
-        r_ref[...] = r
-        yb = y.astype(bf16)
-        for blk in range(4):
-            act, slope = activate(dot_nn(yb, w_ref[:, blk * HID : (blk + 1) * HID]))
-            slope_ref[:, blk * HID : (blk + 1) * HID] = slope
-            if blk == 2:
-                act = act.astype(bf16).astype(f32) * (DH**-0.5)
-            act = act.astype(bf16)
-            if blk == 0:
-                u_ref[...] = act
-            else:
-                for hp in range(PAIRS):
-                    part = act[:, hp * 2 * DH : (hp + 1) * 2 * DH]
-                    if blk == 1:
-                        v_ref[1, hp] = part
-                    elif blk == 2:
-                        q_ref[hp] = part
-                    else:
-                        k_ref[1, hp] = part
+        r_ref[...] = 0.5 * r
+        project(1, (0, 1, 2, 3), (0.5 * y).astype(bf16), slope_ref)
 
         @pl.when(upper)
         def _():
             y, r = norm(features(0))
             yl_ref[...] = y
-            rl_ref[...] = r
-            yb = y.astype(bf16)
-            for n, blk in enumerate((1, 3)):
-                act, slope = activate(dot_nn(yb, w_ref[:, blk * HID : (blk + 1) * HID]))
-                slopel_ref[:, n * HID : (n + 1) * HID] = slope
-                act = act.astype(bf16)
-                for hp in range(PAIRS):
-                    part = act[:, hp * 2 * DH : (hp + 1) * 2 * DH]
-                    if n == 0:
-                        v_ref[0, hp] = part
-                    else:
-                        k_ref[0, hp] = part
-
-        def weights(scores, limit):
-            s = sigmoid(scores)
-            act = scores * s
-            slope = s + act * (1.0 - s)
-            if limit is not None:
-                ok = lax.broadcasted_iota(jnp.int32, scores.shape, 1) <= limit
-                act = jnp.where(ok, act, 0.0)
-                slope = jnp.where(ok, slope, 0.0)
-            return (act * (1.0 / LEN)).astype(bf16), slope * (1.0 / LEN)
-
-        QB = HALF // 2
-        row = lax.broadcasted_iota(jnp.int32, (QB, 1), 0)
-
-        @pl.loop(0, PAIRS)
-        def _(hp):
-            q, k, v = q_ref[hp], k_ref[1, hp], v_ref[1, hp]
-            att = [None, None]
-            for h in range(2):
-                vm = v * head_mask[h]
-                for qi in range(2):
-                    qb = q[qi * QB : (qi + 1) * QB] * head_mask[h]
-                    for ki in range(qi + 1):
-                        scores = dot_nt(qb, k[ki * QB : (ki + 1) * QB])
-                        limit = None
-                        if ki == qi:
-                            limit = jnp.minimum(row, length - 1 - base - ki * QB)
-                        p, d = weights(scores, limit)
-                        at = 2 * qi + ki
-                        p_ref[2 * hp + h, at] = p
-                        d_ref[2 * hp + h, at] = d
-                        add = dot_nn(p, vm[ki * QB : (ki + 1) * QB])
-                        att[qi] = add if att[qi] is None else att[qi] + add
-            att_ref[hp] = jnp.concatenate(att, axis=0)
-
-            @pl.when(upper)
-            def _():
-                kl, vl = k_ref[0, hp], v_ref[0, hp]
-                for h in range(2):
-                    scores = dot_nt(q * head_mask[h], kl)
-                    p, d = weights(scores, None)
-                    pl_ref[2 * hp + h] = p
-                    dl_ref[2 * hp + h] = d
-                    att_ref[hp] += dot_nn(p, vl * head_mask[h])
-
-        att = jnp.concatenate([att_ref[hp] for hp in range(PAIRS)], axis=1)
-        na, ra = norm(att)
+            rl_ref[...] = 0.5 * r
+            project(0, (1, 3), (0.5 * y).astype(bf16), slopel_ref)
+
+        over_pairs(forward)
+
+        na, ra = norm(att_ref[...].T * (1.0 / LEN))
         u = u_ref[...].astype(f32)
         valid = (base + lax.broadcasted_iota(jnp.int32, (HALF, 1), 0)) < length
         mixed = dot_nn((na * u).astype(bf16), wo_ref[...]) + x_ref[...]
@@ -340,64 +372,25 @@
         cot = jnp.where(valid, cot_ref[...].astype(f32), 0.0)
         gg = dot_nt(cot.astype(bf16), wo_ref[...])
         pg_ref[:, :HID] = (gg * na * slope_ref[:, :HID]).astype(bf16)
-        da = norm_back(na, ra, gg * u).astype(bf16)
-        for hp in range(PAIRS):
-            do_ref[hp] = da[:, hp * 2 * DH : (hp + 1) * 2 * DH]
-
-        @pl.loop(0, PAIRS)
-        def _(hp):
-            q, k, v, do = q_ref[hp], k_ref[1, hp], v_ref[1, hp], do_ref[hp]
-            dq = [None, None]
-            dk = [None, None]
-            dv = [None, None]
-
-            def plus(a, b):
-                return b if a is None else a + b
-
-            for h in range(2):
-                km = k * head_mask[h]
-                qm = q * head_mask[h]
-                dm = do * head_mask[h]
-                for qi in range(2):
-                    qs = slice(qi * QB, (qi + 1) * QB)
-                    for ki in range(qi + 1):
-                        ks = slice(ki * QB, (ki + 1) * QB)
-                        at = 2 * qi + ki
-                        ds = (dot_nt(dm[qs], v[ks]) * d_ref[2 * hp + h, at]).astype(bf16)
-                        dq[qi] = plus(dq[qi], dot_nn(ds, km[ks]))
-                        dk[ki] = plus(dk[ki], dot_tn(ds, qm[qs]))
-                        dv[ki] = plus(dv[ki], dot_tn(p_ref[2 * hp + h, at], dm[qs]))
-            at = pl.multiple_of(hp * 2 * DH, 2 * DH)
-            vs = pl.ds(HID + at, 2 * DH)
-            qs_ = pl.ds(2 * HID + at, 2 * DH)
-            ks_ = pl.ds(3 * HID + at, 2 * DH)
-            pg_ref[:, vs] = (jnp.concatenate(dv, axis=0) * slope_ref[:, vs]).astype(bf16)
-            pg_ref[:, ks_] = (jnp.concatenate(dk, axis=0) * slope_ref[:, ks_]).astype(bf16)
-            att_ref[hp] = jnp.concatenate(dq, axis=0)
-
-            @pl.when(upper)
-            def _():
-                kl, vl = k_ref[0, hp], v_ref[0, hp]
-                dkl, dvl = None, None
-                for h in range(2):
-                    dm = do * head_mask[h]
-                    ds = (dot_nt(dm, vl) * dl_ref[2 * hp + h]).astype(bf16)
-                    att_ref[hp] += dot_nn(ds, kl * head_mask[h])
-                    dkl = plus(dkl, dot_tn(ds, q * head_mask[h]))
-                    dvl = plus(dvl, dot_tn(pl_ref[2 * hp + h], dm))
-                vl_ = pl.ds(at, 2 * DH)
-                kl_ = pl.ds(HID + at, 2 * DH)
-                pgl_ref[:, vl_] = (dvl * slopel_ref[:, vl_]).astype(bf16)
-                pgl_ref[:, kl_] = (dkl * slopel_ref[:, kl_]).astype(bf16)
-
-            pg_ref[:, qs_] = (att_ref[hp] * (DH**-0.5) * slope_ref[:, qs_]).astype(bf16)
-
+        da = norm_back(na, ra * (1.0 / LEN), gg * u)
+        dot_ref[...] = da.T.astype(bf16)
+        for hp, part in enumerate(pairs_of(da.astype(bf16))):
+            do_ref[hp] = part
+
+        over_pairs(backward)
+
+        dq = att_ref[...].T * (0.5 * DH**-0.5)
+        pg_ref[:, HID : 2 * HID] = (dv_ref[...].T * slope_ref[:, HID : 2 * HID]).astype(bf16)
+        pg_ref[:, 2 * HID : 3 * HID] = (dq * slope_ref[:, 2 * HID : 3 * HID]).astype(bf16)
+        pg_ref[:, 3 * HID :] = (dk_ref[...].T * slope_ref[:, 3 * HID :]).astype(bf16)
         eg = dot_nt(pg_ref[...], w_ref[...])
         cot = jnp.where(valid, cot_ref[...].astype(f32), 0.0)
         put_grad(seq, cot + norm_back(y_ref[...], r_ref[...], eg))
 
         @pl.when(upper)
         def _():
+            pgl_ref[:, :HID] = (dvl_ref[...].T * slopel_ref[:, :HID]).astype(bf16)
+            pgl_ref[:, HID:] = (dkl_ref[...].T * slopel_ref[:, HID:]).astype(bf16)
             eg = dot_nt(pgl_ref[:, :HID], w_ref[:, HID : 2 * HID])
             eg = eg + dot_nt(pgl_ref[:, HID:], w_ref[:, 3 * HID :])
             put_grad(0, norm_back(yl_ref[...], rl_ref[...], eg))
@@ -480,14 +473,22 @@
             pltpu.VMEM((HALF, 2 * HID), f32),
             pltpu.VMEM((HALF, HID), bf16),
             pltpu.VMEM((PAIRS, HALF, 2 * DH), bf16),
+            pltpu.VMEM((HID, HALF), bf16),
             pltpu.VMEM((2, PAIRS, HALF, 2 * DH), bf16),
+            pltpu.VMEM((2, HID, HALF), bf16),
             pltpu.VMEM((2, PAIRS, HALF, 2 * DH), bf16),
+            pltpu.VMEM((2, HID, HALF), bf16),
             pltpu.VMEM((H, 4, HALF // 2, HALF // 2), bf16),
             pltpu.VMEM((H, 4, HALF // 2, HALF // 2), f32),
             pltpu.VMEM((H, HALF, HALF), bf16),
             pltpu.VMEM((H, HALF, HALF), f32),
-            pltpu.VMEM((PAIRS, HALF, 2 * DH), f32),
+            pltpu.VMEM((HID, HALF), f32),
             pltpu.VMEM((PAIRS, HALF, 2 * DH), bf16),
+            pltpu.VMEM((HID, HALF), bf16),
+            pltpu.VMEM((HID, HALF), f32),
+            pltpu.VMEM((HID, HALF), f32),
+            pltpu.VMEM((HID, HALF), f32),
+            pltpu.VMEM((HID, HALF), f32),
             pltpu.VMEM((HALF, 4 * HID), bf16),
             pltpu.VMEM((HALF, 2 * HID), bf16),
         ],

time: 157 us -> 150 us (0.955); the launches traced: 155 us -> 150 us
  starting transfers between devices: 30.7 us -> 27.4 us
    all_to_all x1, starting transfers between devices: 17 us -> 13.6 us  [per_device(): back = lax.all_to_all(grad, both, split_axis=0, concat_axis=0, tiled=True)]
  transfers between devices with their start and end apart: 4 -> 4, of which waited for: 2 -> 2; matrix products, arithmetic and copies ran while one was open for 0% -> 0% of each run, Pallas kernels for 13% -> 14%
where the time goes in v3:
time: 150 us
  Pallas kernels  78.8 us (53%)
  waiting for transfers between devices  38.4 us (26%)
  starting transfers between devices  27.4 us (18%)
  local copies, waits for them, and re-layouts  2.59 us (2%)
  other arithmetic  2.28 us (2%)
    pallas_call x2, Pallas kernels, scatter(): pl.pallas_call(scatter_kernel, in_specs=[smem(), smem(), smem(), vmem(),...  33.7 us
    pallas_call x1, Pallas kernels, gather(): pl.pallas_call(gather_kernel, in_specs=[smem(), smem(), vmem(), vmem(), v...  21.7 us
    pallas_call x1, Pallas kernels, layer(): pl.pallas_call(layer_kernel, in_specs=[smem(), smem(), smem(), vmem(), vm...  19.9 us
    all_to_all x1, waiting for transfers between devices, per_device(): back = lax.all_to_all(grad, both, split_axis=0, concat_axis=0, tiled=True)  19.2 us
    all_to_all x1, waiting for transfers between devices, per_device(): lax.all_to_all(flat, both, split_axis=0, concat_axis=0, tiled=True)  19.2 us
    all_to_all x1, starting transfers between devices, per_device(): back = lax.all_to_all(grad, both, split_axis=0, concat_axis=0, tiled=True)  13.6 us
    all_to_all x1, starting transfers between devices, per_device(): lax.all_to_all(flat, both, split_axis=0, concat_axis=0, tiled=True)  11.4 us
    pallas_call x1, Pallas kernels, table_rows(): pl.pallas_call(rows_kernel, in_specs=[vmem()], out_specs=vmem(), out_shap...  3.53 us
  transfers between devices with their start and end apart: 4, of which 2 were waited for; matrix products, arithmetic and copies ran while one was open for 0% of the time, Pallas kernels for 14%

profile of v3, /device:TPU:1, one launch (start us, length us, event | category | flops | bytes accessed | tf_op | source)
XLA Modules:
  0.0 150.1 jit_solution(3436491062249627025)
XLA Ops:
  0.6 2.1 %collective-permute-start = (s32[64,512]{1,0:T(8,128)}, s32[64,512]{1,0:T(8,128)S(1)}, u32[]{:S(2)}, u32[]{:S(2)}) collective-permute-start(s32[64,512]{1,0:T(8,128)} %own_ref.5), channel_id=1, source_target_pairs={{0,1},{1,0},{2,3},{3,2},{4,5},{5,4},{6,7},{7,6},{8,9},{9,8},{10,11... | collective-permute-start | bytes 393224 | tf_op jit(solution)/shard_map/ppermute | solution.py:506
  2.7 3.5 %table_rows.1.rows_ref = f32[4096,128]{1,0:T(8,128)} custom-call(f32[8,65536]{1,0:T(8,128)} %table_ref.1), custom_call_target="tpu_custom_call" | custom-call | tf_op jit(solution)/shard_map/table_rows/pallas_call | solution.py:412
  6.3 0.0 collective-permute-done.other_ref
  6.3 0.0 copy-start.2
  6.3 0.7 copy-done.2
  6.9 21.7 %gather.1 = bf16[64,2,8,512]{3,2,1,0:T(8,128)(2,1)} custom-call(s32[1]{0:T(128)} %bitcast.seq_ref.half_ref, s32[64]{0:T(128)} %lengths_ref.7, s32[64,512]{1,0:T(8,128)} %own_ref.5, s32[64,512]{1,0:T(8,128)} %copy-done.2, f32[4096,128]{1,0:T(8,128)} %table_rows.1.rows_ref), custom_call_target="tpu_custom_call" | custom-call | tf_op jit(solution)/shard_map/gather/pallas_call | solution.py:423
  28.6 11.4 %all-to-all-start = ((bf16[128,8,512]{2,1,0:T(8,128)(2,1)}), bf16[128,8,512]{2,1,0:T(8,128)(2,1)S(1)}, u32[]{:S(2)}, u32[]{:S(2)}) async-start(bf16[128,8,512]{2,1,0:T(8,128)(2,1)} %bitcast.11), calls=%async_computation | async-start | bytes 2097152 | tf_op jit(solution)/shard_map/all_to_all | solution.py:510
  40.0 19.2 %all-to-all-done = bf16[128,8,512]{2,1,0:T(8,128)(2,1)S(1)} async-done(((bf16[128,8,512]{2,1,0:T(8,128)(2,1)}), bf16[128,8,512]{2,1,0:T(8,128)(2,1)S(1)}, u32[]{:S(2)}, u32[]{:S(2)}) %all-to-all-start) | async-done | bytes 1048608 | tf_op jit(solution)/shard_map/all_to_all | solution.py:510
  59.2 0.0 copy-start.1
  59.2 1.0 copy-done.1
  60.2 19.9 %layer.1 = (bf16[512,512]{1,0:T(8,128)(2,1)}, bf16[64,2,8,512]{3,2,1,0:T(8,128)(2,1)}) custom-call(s32[1]{0:T(128)} %bitcast.seq_ref.half_ref, s32[1]{0:T(128)} %bitcast.1.col_ref, s32[64]{0:T(128)} %lengths_ref.7, bf16[64,2,8,512]{3,2,1,0:T(8,128)(2,1)} %bitcast.10, bf16[512,2048]{1,0:T(8,128)(2,1)} %w_ref.1, bf16[512,512]{1,0:T(8,128)(2,1)} %wo_ref.1, ...), custom_call_target="tpu_custom_call" | custom-call | tf_op jit(solution)/shard_map/layer/pallas_call | solution.py:458
  80.1 13.6 %all-to-all-start.1 = ((bf16[128,8,512]{2,1,0:T(8,128)(2,1)}), bf16[128,8,512]{2,1,0:T(8,128)(2,1)S(1)}, u32[]{:S(2)}, u32[]{:S(2)}) async-start(bf16[128,8,512]{2,1,0:T(8,128)(2,1)} %bitcast.12), calls=%async_computation.1 | async-start | bytes 2097152 | tf_op jit(solution)/shard_map/all_to_all | solution.py:516
  93.7 19.2 %all-to-all-done.1 = bf16[128,8,512]{2,1,0:T(8,128)(2,1)S(1)} async-done(((bf16[128,8,512]{2,1,0:T(8,128)(2,1)}), bf16[128,8,512]{2,1,0:T(8,128)(2,1)S(1)}, u32[]{:S(2)}, u32[]{:S(2)}) %all-to-all-start.1) | async-done | bytes 1048608 | tf_op jit(solution)/shard_map/all_to_all | solution.py:516
  112.9 0.0 copy-start
  112.9 1.0 copy-done
  113.9 16.8 %scatter.3 = bf16[8,32768]{1,0:T(8,128)(2,1)} custom-call(s32[1]{0:T(128)} %bitcast.seq_ref.half_ref, s32[64]{0:T(128)} %lengths_ref.7, s32[1]{0:T(128)S(6)} %sub.3.half_ref, s32[64,512]{1,0:T(8,128)} %own_ref.5, s32[64,512]{1,0:T(8,128)} %copy-done.2, bf16[64,2,8,512]{3,2,1,0:T(8,128)(2,1)} %bitcast.8), custom_call_target="tpu_custom_call" | custom-call | tf_op jit(solution)/shard_map/scatter/pallas_call | solution.py:442
  130.7 0.3 collective-permute-start.1
  131.0 16.9 %scatter.2 = f32[8,32768]{1,0:T(8,128)} custom-call(s32[1]{0:T(128)} %bitcast.seq_ref.half_ref, s32[64]{0:T(128)} %lengths_ref.7, s32[1]{0:T(128)} %bitcast.seq_ref.half_ref, s32[64,512]{1,0:T(8,128)} %own_ref.5, s32[64,512]{1,0:T(8,128)} %copy-done.2, bf16[64,2,8,512]{3,2,1,0:T(8,128)(2,1)} %bitcast.9), custom_call_target="tpu_custom_call" | custom-call | tf_op jit(solution)/shard_map/scatter/pallas_call | solution.py:442
  147.9 0.0 collective-permute-done.1
  147.9 2.3 %convert_add_fusion = f32[8,32768]{1,0:T(8,128)} fusion(f32[8,32768]{1,0:T(8,128)} %scatter.2, bf16[8,32768]{1,0:T(8,128)(2,1)S(1)} %collective-permute-done.1), kind=kLoop, calls=%fused_computation | loop fusion | flops 524288 | bytes 2621440 | tf_op jit(solution)/shard_map/add | solution.py:521
Async XLA Ops:
  0.6 5.6 %collective-permute-start = (s32[64,512]{1,0:T(8,128)}, s32[64,512]{1,0:T(8,128)S(1)}, u32[]{:S(2)}, u32[]{:S(2)}) collective-permute-start(s32[64,512]{1,0:T(8,128)} %own_ref.5), channel_id=1, source_target_pairs={{0,1},{1,0},{2,3},{3,2},{4,5},{5,4},{6,7},{7,6},{8,9},{9,8},{10,11... | collective-permute-start | bytes 393224 | tf_op jit(solution)/shard_map/ppermute | solution.py:506
  6.3 0.7 copy-start.2
  28.6 30.6 %all-to-all-start = ((bf16[128,8,512]{2,1,0:T(8,128)(2,1)}), bf16[128,8,512]{2,1,0:T(8,128)(2,1)S(1)}, u32[]{:S(2)}, u32[]{:S(2)}) async-start(bf16[128,8,512]{2,1,0:T(8,128)(2,1)} %bitcast.11), calls=%async_computation | async-start | bytes 2097152 | tf_op jit(solution)/shard_map/all_to_all | solution.py:510
  59.2 1.0 copy-start.1
  80.1 32.8 %all-to-all-start.1 = ((bf16[128,8,512]{2,1,0:T(8,128)(2,1)}), bf16[128,8,512]{2,1,0:T(8,128)(2,1)S(1)}, u32[]{:S(2)}, u32[]{:S(2)}) async-start(bf16[128,8,512]{2,1,0:T(8,128)(2,1)} %bitcast.12), calls=%async_computation.1 | async-start | bytes 2097152 | tf_op jit(solution)/shard_map/all_to_all | solution.py:516
  112.9 1.0 copy-start
  130.7 17.2 %collective-permute-start.1 = (bf16[8,32768]{1,0:T(8,128)(2,1)}, bf16[8,32768]{1,0:T(8,128)(2,1)S(1)}, u32[]{:S(2)}, u32[]{:S(2)}) collective-permute-start(bf16[8,32768]{1,0:T(8,128)(2,1)} %scatter.3), channel_id=1, source_target_pairs={{0,1},{1,0},{2,3},{3,2},{4,5},{5,4},{6,7},{7,6},{8,9},{9,8},{10,11... | collective-permute-start | bytes 1572872 | tf_op jit(solution)/shard_map/ppermute | solution.py:519
